TPU v7x, 256 devices: a whole 4x4x8 slice. The times are simulated.
256 devices in a mesh: dp: 16 (over y, x), seq: 16 (over z, core).
Axes of the slice: x: 4, y: 4, z: 8, core: 2. Of those that a mesh axis runs over, the one named last changes fastest.
Arguments:
- query_states: bfloat16 [16, 2048, 5120], P('dp', 'seq'), may hold values from -36 to 36
- key_states: bfloat16 [16, 2048, 1024], P('dp', 'seq'), may hold values from -3 to 3
- value_states: bfloat16 [16, 2048, 1024], P('dp', 'seq'), may hold values from -6 to 6
- output_grad: bfloat16 [16, 2048, 5120], P('dp', 'seq'), may hold values from -6 to 6
- layer_input: bfloat16 [16, 2048, 4096], P('dp', 'seq'), may hold values from -6 to 6
- head_counts: int32 [8], replicated, may hold values from 1 to 8, 40 in all
Outputs:
- query_grad: bfloat16 [16, 2048, 5120], P('dp', 'seq')
- key_grad: bfloat16 [16, 2048, 1024], P('dp', 'seq')
- weight_grad: float32 [4096, 512], P(('dp', 'seq'))
Inputs may be any that keep to these rules, and one draw needn't show every extreme that they name: `head_counts`: kept query heads of each of the 8 groups; they sum to 40, and some group keeps all 8.
All inputs are finite; a program needn't handle non-finite values.
Results may differ from a plain program's by a relative error of at most 0.0085.
Values may be sent and summed in bfloat16 or wider, within the bound.
A program may use at most 128 MiB of HBM per device.

v0:
```python
import math

import jax
import jax.numpy as jnp
from jax import lax
from jax.sharding import PartitionSpec as P

HD = 128
KVG = 8
QPG = 8
HKEPT = 40
VGW = 4


masked_score = -1e30


def shortened(value):

    def short(part):
        return part.astype(jnp.bfloat16) if part.dtype == jnp.float32 else part

    return jax.tree.map(short, value)


def head_pass(queries, key_rows, value_rows, grad_rows):
    sequence = queries.shape[0]
    head_width = queries.shape[1]
    scaling = 1.0 / math.sqrt(head_width)
    block_rows = min(512, sequence)
    grad_blocks = []
    key_total = jnp.zeros((sequence, head_width), jnp.float32)
    value_total = jnp.zeros((sequence, head_width), jnp.float32)
    for number in range(sequence // block_rows):
        row_start = number * block_rows
        row_end = row_start + block_rows
        query_block = queries[row_start:row_end]
        grad_block = grad_rows[row_start:row_end]
        key_part = key_rows[:row_end]
        value_part = value_rows[:row_end]
        scores = (
            lax.dot_general(
                query_block, key_part, (((1,), (1,)), ((), ())), preferred_element_type=jnp.float32
            )
            * scaling
        )
        row_position = row_start + lax.broadcasted_iota(jnp.int32, (block_rows, row_end), 0)
        column_position = lax.broadcasted_iota(jnp.int32, (block_rows, row_end), 1)
        scores = jnp.where(column_position <= row_position, scores, masked_score)
        top_score = jnp.max(scores, axis=1, keepdims=True)
        weights = jnp.exp(scores - top_score)
        softmax_rows = weights / jnp.sum(weights, axis=1, keepdims=True)
        softmax_half = softmax_rows.astype(jnp.bfloat16)
        grad_weights = lax.dot_general(
            grad_block, value_part, (((1,), (1,)), ((), ())), preferred_element_type=jnp.float32
        )
        row_terms = jnp.sum(softmax_rows * grad_weights, axis=1, keepdims=True)
        grad_scores = (softmax_rows * (grad_weights - row_terms) * scaling).astype(jnp.bfloat16)
        grad_blocks.append(
            jnp.dot(grad_scores, key_part, preferred_element_type=jnp.float32).astype(jnp.bfloat16)
        )
        key_step = lax.dot_general(
            grad_scores, query_block, (((0,), (0,)), ((), ())), preferred_element_type=jnp.float32
        )
        value_step = lax.dot_general(
            softmax_half, grad_block, (((0,), (0,)), ((), ())), preferred_element_type=jnp.float32
        )
        key_total = key_total.at[:row_end].add(key_step)
        value_total = value_total.at[:row_end].add(value_step)
    return (
        jnp.concatenate(grad_blocks, axis=0),
        key_total.astype(jnp.bfloat16),
        value_total.astype(jnp.bfloat16),
    )


def local(query_states, key_states, value_states, output_grad, layer_input, head_counts):
    devices = lax.axis_size("seq")
    token_count = query_states.shape[1]
    sequence = token_count * devices
    queries_local = query_states[0].reshape(token_count, HKEPT, HD)
    grads_local = output_grad[0].reshape(token_count, HKEPT, HD)
    keys_local = key_states[0].reshape(token_count, KVG, HD)
    values_local = value_states[0].reshape(token_count, KVG, HD)
    head_index = jnp.arange(HKEPT, dtype=jnp.int32)
    group_ends = jnp.cumsum(head_counts)
    group_of = jnp.sum((group_ends[None, :] <= head_index[:, None]).astype(jnp.int32), axis=1)
    group_hot = group_of[:, None] == jnp.arange(KVG, dtype=jnp.int32)[None, :]
    starts = group_ends - head_counts
    rank_in_group = head_index - jnp.sum(jnp.where(group_hot, starts[None, :], 0), axis=1)
    per_group = devices // KVG
    slot_count = (QPG * KVG + devices - 1) // devices
    head_owner = group_of * per_group + rank_in_group % per_group
    slot_index = rank_in_group // per_group
    slot_match = slot_index[:, None, None] == jnp.arange(slot_count, dtype=jnp.int32)[None, :, None]
    owner_match = head_owner[:, None, None] == jnp.arange(devices, dtype=jnp.int32)[None, None, :]
    select = (slot_match & owner_match).astype(jnp.bfloat16)
    query_send = jnp.einsum(
        "hsd,thc->sdtc", select, queries_local, preferred_element_type=jnp.float32
    ).astype(jnp.bfloat16)
    grad_send = jnp.einsum(
        "hsd,thc->sdtc", select, grads_local, preferred_element_type=jnp.float32
    ).astype(jnp.bfloat16)
    group_states = (
        lax.all_to_all(
            jnp.repeat(keys_local, per_group, axis=1),
            "seq",
            split_axis=1,
            concat_axis=0,
            tiled=True,
        ),
        lax.all_to_all(
            jnp.repeat(values_local, per_group, axis=1),
            "seq",
            split_axis=1,
            concat_axis=0,
            tiled=True,
        ),
    )
    key_sequence = group_states[0].reshape(sequence, HD)
    value_sequence = group_states[1].reshape(sequence, HD)

    def grouped_head(item):
        return head_pass(item[0], key_sequence, value_sequence, item[1])

    pieces = (
        lax.all_to_all(query_send, "seq", split_axis=1, concat_axis=1, tiled=True),
        lax.all_to_all(grad_send, "seq", split_axis=1, concat_axis=1, tiled=True),
    )
    item_count = pieces[0].shape[0]
    query_items = pieces[0].reshape(item_count, sequence, HD)
    grad_items = pieces[1].reshape(item_count, sequence, HD)
    head_results = lax.map(grouped_head, (query_items, grad_items))
    query_returned = lax.all_to_all(
        shortened(head_results[0].reshape(slot_count, devices, token_count, HD)),
        "seq",
        split_axis=1,
        concat_axis=1,
        tiled=True,
    )
    key_partial = jnp.sum(head_results[1].astype(jnp.float32), axis=0).reshape(
        devices, token_count, HD
    )
    value_partial = jnp.sum(head_results[2].astype(jnp.float32), axis=0).reshape(
        devices, token_count, HD
    )
    group_returned = (
        lax.all_to_all(
            key_partial.astype(jnp.bfloat16), "seq", split_axis=0, concat_axis=0, tiled=True
        ).astype(key_partial.dtype),
        lax.all_to_all(
            value_partial.astype(jnp.bfloat16), "seq", split_axis=0, concat_axis=0, tiled=True
        ).astype(value_partial.dtype),
    )
    key_grad = jnp.sum(group_returned[0].reshape(KVG, per_group, token_count, HD), axis=1)
    value_grad = jnp.sum(group_returned[1].reshape(KVG, per_group, token_count, HD), axis=1)
    key_grad = key_grad.transpose(1, 0, 2).reshape(token_count, KVG * HD)
    value_grad = value_grad.transpose(1, 0, 2).reshape(token_count, KVG * HD)
    query_grad = jnp.einsum(
        "sdtc,hsd->thc", query_returned, select, preferred_element_type=jnp.float32
    ).astype(jnp.bfloat16)
    query_grad = query_grad.reshape(1, token_count, HKEPT * HD)
    key_result = key_grad.astype(jnp.bfloat16).reshape(1, token_count, KVG * HD)
    value_half = value_grad.astype(jnp.bfloat16)[:, : VGW * HD]
    layer_rows = layer_input[0]
    weight_grad = lax.psum_scatter(
        lax.dot_general(
            layer_rows, value_half, (((0,), (0,)), ((), ())), preferred_element_type=jnp.float32
        ),
        ("dp", "seq"),
        scatter_dimension=0,
        tiled=True,
    )
    return (query_grad, key_result, weight_grad)


def solution(mesh):
    placed = (
        P("dp", "seq", None),
        P("dp", "seq", None),
        P("dp", "seq", None),
        P("dp", "seq", None),
        P("dp", "seq", None),
        P(),
    )
    return jax.shard_map(
        local,
        mesh=mesh,
        in_specs=placed,
        out_specs=(P("dp", "seq", None), P("dp", "seq", None), P(("dp", "seq"), None)),
        check_vma=False,
    )
```

profile of v0, /device:TPU:1, one launch (start us, length us, event | category | flops | bytes accessed | tf_op | source)
XLA Modules:
  0.0 1629.4 jit_solution(704380425249459751)
XLA Ops:
  9.3 10.0 all-to-all-start.1
  20.7 1.9 copy.37
  22.6 13.9 all-to-all-done.1
  36.5 4.3 all-to-all-start
  41.8 1.9 copy.40
  43.7 44.7 %all-to-all-done = bf16[4,16,128,128]{3,2,0,1:T(8,128)(2,1)} async-done(((bf16[4,16,128,128]{3,2,0,1:T(8,128)(2,1)}), bf16[4,16,128,128]{3,2,0,1:T(8,128)(2,1)}, u32[]{:S(2)}, u32[]{:S(2)}) %all-to-all-start) | async-done | bytes 2097184 | tf_op jit(solution)/shard_map/all_to_all | solution.py:127
  88.4 5.1 all-to-all-start.2
  93.6 49.1 %all-to-all-done.2 = bf16[4,16,128,128]{3,2,0,1:T(8,128)(2,1)} async-done(((bf16[4,16,128,128]{3,2,0,1:T(8,128)(2,1)}), bf16[4,16,128,128]{3,2,0,1:T(8,128)(2,1)}, u32[]{:S(2)}, u32[]{:S(2)}) %all-to-all-start.2) | async-done | bytes 2097184 | tf_op jit(solution)/shard_map/all_to_all | solution.py:128
  143.6 4.8 all-to-all-start.3
  148.5 3.2 copy.38
  151.7 3.1 copy.41
  154.8 10.8 all-to-all-done.3
  165.6 119.3 %while.27 = (s32[]{:T(128)}, bf16[4,2048,128]{2,1,0:T(8,128)(2,1)}, bf16[4,2048,128]{2,1,0:T(8,128)(2,1)}, bf16[4,2048,128]{2,1,0:T(8,128)(2,1)}, bf16[4,2048,12...) while((s32[]{:T(128)}, bf16[4,2048,128]{2,1,0:T(8,128)(2,1)}, ...), condition=%wide.region_16.17_spmd, body=%wide.region_3.16_spmd.sunk | while | flops 3409309184 | bytes 116759848 | solution.py:133
  170.0 1.5 fusion.150
  174.2 1.4 fusion.156
  176.1 1.7 fusion.148
  181.3 1.6 fusion.157
  183.5 1.9 fusion.146
  186.1 2.3 fusion.162
  188.4 1.5 multiply_reduce_fusion.8
  189.9 1.5 multiply_convert_fusion.8
  192.1 2.5 fusion.158
  195.4 1.4 fusion.152
  199.7 1.5 fusion.150
  203.9 1.4 fusion.156
  205.8 1.7 fusion.148
  211.1 1.6 fusion.157
  213.3 1.9 fusion.146
  215.9 2.3 fusion.162
  218.2 1.5 multiply_reduce_fusion.8
  219.7 1.5 multiply_convert_fusion.8
  221.9 2.5 fusion.158
  229.6 1.5 fusion.150
  233.8 1.4 fusion.156
  235.7 1.7 fusion.148
  240.9 1.6 fusion.157
  243.1 1.9 fusion.146
  245.7 2.3 fusion.162
  248.0 1.5 multiply_reduce_fusion.8
  249.5 1.5 multiply_convert_fusion.8
  251.7 2.5 fusion.158
  259.4 1.5 fusion.150
  263.6 1.4 fusion.156
  265.5 1.7 fusion.148
  270.7 1.6 fusion.157
  272.9 1.9 fusion.146
  275.5 2.3 fusion.162
  277.8 1.5 multiply_reduce_fusion.8
  279.3 1.5 multiply_convert_fusion.8
  281.5 2.5 fusion.158
  284.9 2.2 reduce_sum.168
  287.1 20.0 %all_to_all.55 = bf16[16,128,128]{2,1,0:T(8,128)(2,1)S(1)} all-to-all(bf16[16,128,128]{2,1,0:T(8,128)(2,1)S(1)} %bitcast.205), channel_id=1, replica_groups=mesh['dp'=16,'seq'=16] {'seq'}, dimensions={0} | all-to-all | bytes 1048576 | tf_op jit(solution)/shard_map/all_to_all | solution.py:151
  307.3 4.5 convolution_bitcast_fusion
  311.8 9.0 copy.51
  320.8 1.6 copy-done.2
  323.6 3.5 all-to-all-start.5
  327.1 4.8 copy.43
  331.9 12.5 all-to-all-done.5
  345.2 3.6 all-to-all-start.4
  350.8 1.8 copy.47
  352.5 46.2 %all-to-all-done.4 = bf16[4,16,128,128]{3,0,2,1:T(4,128)(2,1)S(1)} async-done(((bf16[4,16,128,128]{3,0,2,1:T(4,128)(2,1)}), bf16[4,16,128,128]{3,0,2,1:T(4,128)(2,1)S(1)}, u32[]{:S(2)}, u32[]{:S(2)}) %all-to-all-start.4) | async-done | bytes 2097184 | tf_op jit(solution)/shard_map/all_to_all | solution.py:134
  398.7 2.8 fusion.64
  401.5 3.2 reshape.431
  404.7 1217.8 %reduce-scatter.4.cloned.1.call-done = f32[16,512]{1,0:T(8,128)} async-done(((f32[4096,512]{1,0:T(8,128)}), f32[16,512]{1,0:T(8,128)}) %reduce-scatter.4.cloned.1.call-update) | async-done | bytes 32784
  (155 shorter events, 63.5 us)
Async XLA Ops:
  7.2 300.2 %copy-start = (bf16[1,128,4096]{2,1,0:T(8,128)(2,1)S(1)}, bf16[1,128,4096]{2,1,0:T(8,128)(2,1)}, u32[]{:S(2)}) copy-start(bf16[1,128,4096]{2,1,0:T(8,128)(2,1)} %param.32) | copy-start | bytes 3145732
  7.2 12.1 copy-start.11
  7.2 12.4 copy-start.4
  9.3 27.2 %all-to-all-start.1 = ((bf16[128,16,128]{2,0,1:T(8,128)(2,1)}), bf16[128,16,128]{2,0,1:T(8,128)(2,1)S(1)}, u32[]{:S(2)}, u32[]{:S(2)}) async-start(bf16[128,16,128]{2,0,1:T(8,128)(2,1)} %bitcast.16), calls=%async_computation.1 | async-start | bytes 1048576 | tf_op jit(solution)/shard_map/all_to_all | solution.py:105
  19.9 21.2 %copy-start.9 = (pred[40,4]{0,1:T(4,128)(4,1)}, pred[40,4]{0,1:T(4,128)(4,1)S(1)}, u32[]{:S(2)}) copy-start(pred[40,4]{0,1:T(4,128)(4,1)S(1)} %iota_compare_fusion.7) | copy-start | bytes 484
  20.0 21.1 %copy-start.7 = (pred[40,16]{0,1:T(8,128)(4,1)}, pred[40,16]{0,1:T(8,128)(4,1)S(1)}, u32[]{:S(2)}) copy-start(pred[40,16]{0,1:T(8,128)(4,1)S(1)} %iota_compare_fusion.4) | copy-start | bytes 1924
  22.6 18.2 %copy-start.5 = (bf16[1,128,5120]{2,1,0:T(8,128)(2,1)S(1)}, bf16[1,128,5120]{2,1,0:T(8,128)(2,1)}, u32[]{:S(2)}) copy-start(bf16[1,128,5120]{2,1,0:T(8,128)(2,1)} %param.31) | copy-start | bytes 3932164
  36.5 51.9 %all-to-all-start = ((bf16[4,16,128,128]{3,2,0,1:T(8,128)(2,1)}), bf16[4,16,128,128]{3,2,0,1:T(8,128)(2,1)}, u32[]{:S(2)}, u32[]{:S(2)}) async-start(bf16[4,16,128,128]{3,2,0,1:T(8,128)(2,1)} %copy.37), calls=%async_computation | async-start | bytes 4194304 | tf_op jit(solution)/shard_map/all_to_all | solution.py:127
  43.7 49.8 %copy-start.6 = (bf16[1,128,1024]{2,1,0:T(8,128)(2,1)S(1)}, bf16[1,128,1024]{2,1,0:T(8,128)(2,1)}, u32[]{:S(2)}) copy-start(bf16[1,128,1024]{2,1,0:T(8,128)(2,1)} %param.30) | copy-start | bytes 786436
  88.4 54.3 %all-to-all-start.2 = ((bf16[4,16,128,128]{3,2,0,1:T(8,128)(2,1)}), bf16[4,16,128,128]{3,2,0,1:T(8,128)(2,1)}, u32[]{:S(2)}, u32[]{:S(2)}) async-start(bf16[4,16,128,128]{3,2,0,1:T(8,128)(2,1)} %copy.40), calls=%async_computation.2 | async-start | bytes 4194304 | tf_op jit(solution)/shard_map/all_to_all | solution.py:128
  143.6 22.1 %all-to-all-start.3 = ((bf16[128,16,128]{2,0,1:T(8,128)(2,1)}), bf16[128,16,128]{2,0,1:T(8,128)(2,1)S(1)}, u32[]{:S(2)}, u32[]{:S(2)}) async-start(bf16[128,16,128]{2,0,1:T(8,128)(2,1)} %bitcast.22), calls=%async_computation.3 | async-start | bytes 1048576 | tf_op jit(solution)/shard_map/all_to_all | solution.py:112
  148.4 1474.1 %reduce-scatter.4.cloned.1.call-start = ((), (), s32[]{:S(2)}) async-start(), calls=%async_computation.8 | async-start | bytes 8421376
  165.6 1.7 copy-start.1
  195.4 1.7 copy-start.1
  225.3 1.7 copy-start.1
  255.1 1.7 copy-start.1
  320.8 1.6 copy-start.2
  323.6 20.7 %all-to-all-start.5 = ((bf16[16,128,128]{2,1,0:T(8,128)(2,1)}), bf16[16,128,128]{2,1,0:T(8,128)(2,1)S(1)}, u32[]{:S(2)}, u32[]{:S(2)}) async-start(bf16[16,128,128]{2,1,0:T(8,128)(2,1)} %bitcast.204), calls=%async_computation.5 | async-start | bytes 1048576 | tf_op jit(solution)/shard_map/all_to_all | solution.py:148
  331.9 66.8 %copy-start.8 = (pred[40,16]{0,1:T(8,128)(4,1)S(1)}, pred[40,16]{0,1:T(8,128)(4,1)}, u32[]{:S(2)}) copy-start(pred[40,16]{0,1:T(8,128)(4,1)} %copy-done.7) | copy-start | bytes 1924
  331.9 66.8 %copy-start.10 = (pred[40,4]{0,1:T(4,128)(4,1)S(1)}, pred[40,4]{0,1:T(4,128)(4,1)}, u32[]{:S(2)}) copy-start(pred[40,4]{0,1:T(4,128)(4,1)} %copy-done.9) | copy-start | bytes 484
  344.4 0.8 copy-start.3
  345.2 53.5 %all-to-all-start.4 = ((bf16[4,16,128,128]{3,0,2,1:T(4,128)(2,1)}), bf16[4,16,128,128]{3,0,2,1:T(4,128)(2,1)S(1)}, u32[]{:S(2)}, u32[]{:S(2)}) async-start(bf16[4,16,128,128]{3,0,2,1:T(4,128)(2,1)} %copy.43), calls=%async_computation.4 | async-start | bytes 4194304 | tf_op jit(solution)/shard_map/all_to_all | solution.py:134
Sparse Core Ops, SparseCore 0:
  320.9 1301.5 reduce-scatter.3
where the time goes:
time: 1630 us
  waiting for transfers between devices  1390 us (85%)
  matrix products  102 us (6%)
  local copies, waits for them, and re-layouts  36.7 us (2%)
  starting transfers between devices  31.4 us (2%)
  other arithmetic  29.7 us (2%)
  blocking collectives  20 us (1%)
    unnamed x2, waiting for transfers between devices  1220 us
    all_to_all x1, waiting for transfers between devices, local(): lax.all_to_all(grad_send, 'seq', split_axis=1, concat_axis=1, tiled=True)  49.1 us
    all_to_all x1, waiting for transfers between devices, local(): lax.all_to_all(shortened(head_results[0].reshape(slot_count, devices, tok...  46.2 us
    all_to_all x1, waiting for transfers between devices, local(): lax.all_to_all(query_send, 'seq', split_axis=1, concat_axis=1, tiled=True)  44.7 us
  transfers between devices with their start and end apart: 7, of which 7 were waited for; matrix products, arithmetic and copies ran while one was open for 2% of the time, Pallas kernels for 0%

commit v1 on v0

v1 whole, which is shorter than its diff:
```python
import functools
import math

import jax
import jax.numpy as jnp
from jax import lax
from jax.experimental import pallas as pl
from jax.experimental.pallas import tpu as pltpu
from jax.sharding import PartitionSpec as P

HD = 128
KVG = 8
HKEPT = 40
VGW = 4
CHUNK = 512

masked_score = -1e30
NT = (((1,), (1,)), ((), ()))
NN = (((1,), (0,)), ((), ()))


def matmul(a, b, dims):
    return lax.dot_general(a, b, dims, preferred_element_type=jnp.float32)


def fold_rows(x, op):
    rows, columns = x.shape
    return op(x.reshape(rows // 8, 8, columns), axis=0)


def attention_kernel(
    info, q_ref, do_ref, kv_ref, dq_ref, dkv_ref,
    qs, dos, s_scr, dp_scr, acc, kt_scr,
):
    group = pl.program_id(0)
    block = info[2 * KVG]
    first_head = info[group]
    head_count = info[KVG + group]
    tokens = q_ref.shape[0]
    scaling = 1.0 / math.sqrt(HD)
    to_exp2 = scaling * math.log2(math.e)
    last = (block * tokens) // CHUNK
    row_base = block * tokens

    def rows_at(c):
        return pl.ds(pl.multiple_of(c * CHUNK, CHUNK), CHUNK)

    def prepare(c, _):
        rows = rows_at(c)
        kt_scr[:, rows] = kv_ref[rows, :HD].T
        acc[rows, :] = jnp.zeros((CHUNK, 2 * HD), jnp.float32)
        return 0

    lax.fori_loop(0, last + 1, prepare, 0)

    def run_heads(head, count):
        width = count * tokens
        for i in range(count):
            columns = pl.ds(pl.multiple_of((head + i) * HD, HD), HD)
            qs[i * tokens:(i + 1) * tokens, :] = q_ref[:, columns]
            dos[i * tokens:(i + 1) * tokens, :] = do_ref[:, columns]
        q = qs[:width, :]
        do = dos[:width, :]

        def scores(c, top, masked):
            rows = rows_at(c)
            s = matmul(kv_ref[rows, :HD], q, NT)
            if masked:
                key_at = c * CHUNK + lax.broadcasted_iota(jnp.int32, (CHUNK, width), 0)
                row_at = row_base + lax.rem(
                    lax.broadcasted_iota(jnp.int32, (CHUNK, width), 1), tokens
                )
                s = jnp.where(key_at <= row_at, s, masked_score)
            s_scr[rows, :width] = s
            return jnp.maximum(top, fold_rows(s, jnp.max))

        top = lax.fori_loop(
            0, last, lambda c, t: scores(c, t, False),
            jnp.full((8, width), masked_score, jnp.float32),
        )
        top = scores(last, top, True)
        shift = jnp.max(top, axis=0, keepdims=True) * to_exp2

        def weigh(c, carry):
            total, term = carry
            rows = rows_at(c)
            e = jnp.exp2(s_scr[rows, :width] * to_exp2 - shift)
            dp = matmul(kv_ref[rows, HD:], do, NT)
            s_scr[rows, :width] = e
            dp_scr[rows, :width] = dp
            return (total + fold_rows(e, jnp.sum), term + fold_rows(e * dp, jnp.sum))

        zero = jnp.zeros((8, width), jnp.float32)
        total, term = lax.fori_loop(0, last + 1, weigh, (zero, zero))
        inverse = 1.0 / jnp.sum(total, axis=0, keepdims=True)
        row_term = jnp.sum(term, axis=0, keepdims=True) * inverse

        def grads(c, dqt):
            rows = rows_at(c)
            p = s_scr[rows, :width] * inverse
            ds = (p * (dp_scr[rows, :width] - row_term)).astype(jnp.bfloat16)
            acc[rows, HD:] += matmul(p.astype(jnp.bfloat16), do, NN)
            acc[rows, :HD] += matmul(ds, q, NN)
            return dqt + matmul(kt_scr[:, rows], ds, NN)

        dqt = lax.fori_loop(0, last + 1, grads, jnp.zeros((HD, width), jnp.float32))
        dq = ((dqt * scaling).T).astype(dq_ref.dtype)
        for i in range(count):
            columns = pl.ds(pl.multiple_of((head + i) * HD, HD), HD)
            dq_ref[:, columns] = dq[i * tokens:(i + 1) * tokens, :]

    def pair(i, _):
        run_heads(first_head + 2 * i, 2)
        return 0

    lax.fori_loop(0, head_count // 2, pair, 0)

    @pl.when(head_count % 2 == 1)
    def _():
        run_heads(first_head + head_count - 1, 1)

    def finish(c, _):
        rows = rows_at(c)
        dkv_ref[rows, :HD] = (acc[rows, :HD] * scaling).astype(dkv_ref.dtype)
        dkv_ref[rows, HD:] = acc[rows, HD:].astype(dkv_ref.dtype)
        return 0

    lax.fori_loop(0, last + 1, finish, 0)

    def clear(c, _):
        dkv_ref[rows_at(c), :] = jnp.zeros((CHUNK, 2 * HD), dkv_ref.dtype)
        return 0

    lax.fori_loop(last + 1, dkv_ref.shape[0] // CHUNK, clear, 0)


def attention_grads(queries, grads, kv, info):
    tokens, width = queries.shape
    sequence = kv.shape[0]
    whole = pl.BlockSpec((tokens, width), lambda g, info: (0, 0))
    group_block = pl.BlockSpec((sequence, 2 * HD), lambda g, info: (0, g))
    return pl.pallas_call(
        attention_kernel,
        out_shape=(
            jax.ShapeDtypeStruct((tokens, width), jnp.bfloat16),
            jax.ShapeDtypeStruct(kv.shape, jnp.bfloat16),
        ),
        grid_spec=pltpu.PrefetchScalarGridSpec(
            num_scalar_prefetch=1,
            grid=(KVG,),
            in_specs=[whole, whole, group_block],
            out_specs=[whole, group_block],
            scratch_shapes=[
                pltpu.VMEM((2 * tokens, HD), jnp.bfloat16),
                pltpu.VMEM((2 * tokens, HD), jnp.bfloat16),
                pltpu.VMEM((sequence, 2 * tokens), jnp.float32),
                pltpu.VMEM((sequence, 2 * tokens), jnp.float32),
                pltpu.VMEM((sequence, 2 * HD), jnp.float32),
                pltpu.VMEM((HD, sequence), jnp.bfloat16),
            ],
        ),
        compiler_params=pltpu.CompilerParams(
            dimension_semantics=("arbitrary",), vmem_limit_bytes=48 * 1024 * 1024
        ),
        cost_estimate=pl.CostEstimate(
            flops=2 * 5 * HKEPT * tokens * sequence * HD,
            bytes_accessed=30 * 1024 * 1024,
            transcendentals=HKEPT * tokens * sequence,
        ),
        name="attention_grads",
    )(info, queries, grads, kv)


def local(query_states, key_states, value_states, output_grad, layer_input, head_counts):
    tokens = query_states.shape[1]
    input_parts = lax.all_to_all(
        layer_input, "dp", split_axis=2, concat_axis=0, tiled=True
    )
    keys = key_states[0].reshape(tokens, KVG, 1, HD)
    values = value_states[0].reshape(tokens, KVG, 1, HD)
    kv_local = jnp.concatenate([keys, values], axis=2).reshape(tokens, 2 * KVG * HD)
    kv = lax.all_gather(kv_local, "seq", axis=0, tiled=True)
    group_ends = jnp.cumsum(head_counts)
    info = jnp.concatenate(
        [group_ends - head_counts, head_counts, lax.axis_index("seq").reshape(1)]
    ).astype(jnp.int32)
    query_grad, dkv = attention_grads(query_states[0], output_grad[0], kv, info)
    summed = lax.psum_scatter(dkv, "seq", scatter_dimension=0, tiled=True)
    summed = summed.reshape(tokens, KVG, 2, HD)
    key_grad = summed[:, :, 0, :].reshape(1, tokens, KVG * HD)
    value_window = summed[:, :VGW, 1, :].reshape(1, tokens, VGW * HD)
    value_all = lax.all_gather(value_window, "dp", axis=0, tiled=True)
    weight_part = lax.dot_general(
        input_parts.reshape(-1, input_parts.shape[2]),
        value_all.reshape(-1, VGW * HD),
        (((0,), (0,)), ((), ())),
        preferred_element_type=jnp.float32,
    )
    weight_grad = lax.psum_scatter(weight_part, "seq", scatter_dimension=0, tiled=True)
    return (query_grad[None], key_grad, weight_grad)


def solution(mesh):
    placed = P("dp", "seq", None)
    return jax.shard_map(
        local,
        mesh=mesh,
        in_specs=(placed, placed, placed, placed, placed, P()),
        out_specs=(placed, placed, P(("dp", "seq"), None)),
        check_vma=False,
    )
```

time: 1630 us -> 350 us (0.21)
  waiting for transfers between devices: 1390 us -> 241 us
  matrix products: 102 us -> 2.39 us
  starting transfers between devices: 31.4 us -> 0.16 us
  Pallas kernels: 0 us -> 26.8 us
  local copies, waits for them, and re-layouts: 36.7 us -> 15.2 us
    unnamed x2 -> x5, waiting for transfers between devices: 1220 us -> 52.5 us
    all_to_all x6 -> x0, waiting for transfers between devices: 177 us -> none  [the longest x1 49.1 us: local(): lax.all_to_all(grad_send, 'seq', split_axis=1, concat_axis=1, tiled=True)]
    reduce_scatter x0 -> x1, waiting for transfers between devices: none -> 122 us  [local(): summed = lax.psum_scatter(dkv, 'seq', scatter_dimension=0, tiled=True)]
    dot_general x84 -> x1, matrix products: 102 us -> 2.39 us  [local(): lax.dot_general(input_parts.reshape(-1, input_parts.shape[2]), value_all....]
    all_gather x0 -> x2, waiting for transfers between devices: none -> 66.6 us  [the longest x1 59.9 us: local(): kv = lax.all_gather(kv_local, 'seq', axis=0, tiled=True)]
    all_to_all x6 -> x0, starting transfers between devices: 31.4 us -> none  [the longest x1 9.97 us: local(): lax.all_to_all(jnp.repeat(keys_local, per_group, axis=1), 'seq', split_ax...]
    pallas_call x0 -> x1, Pallas kernels: none -> 26.8 us  [attention_grads(): pl.pallas_call(attention_kernel, out_shape=(jax.ShapeDtypeStruct((tokens,...]
    unnamed x0 -> x1, other arithmetic: none -> 22.4 us
  transfers between devices with their start and end apart: 7 -> 4, of which waited for: 7 -> 4; matrix products, arithmetic and copies ran while one was open for 2% -> 8% of each run, Pallas kernels for 0% -> 0%
where the time goes in v1:
time: 350 us; the launch traced here: 347 us
  waiting for transfers between devices  241 us (69%)
  Pallas kernels  26.8 us (8%)
  other arithmetic  24.9 us (7%)
  blocking collectives  23.1 us (7%)
  local copies, waits for them, and re-layouts  15.2 us (4%)
  between operations  13.9 us (4%)
    reduce_scatter x1, waiting for transfers between devices, local(): summed = lax.psum_scatter(dkv, 'seq', scatter_dimension=0, tiled=True)  122 us
    all_gather x1, waiting for transfers between devices, local(): kv = lax.all_gather(kv_local, 'seq', axis=0, tiled=True)  59.9 us
    unnamed x5, waiting for transfers between devices  52.5 us
    pallas_call x1, Pallas kernels, attention_grads(): pl.pallas_call(attention_kernel, out_shape=(jax.ShapeDtypeStruct((tokens,...  26.8 us
    all_to_all x1, blocking collectives, local(): lax.all_to_all(layer_input, 'dp', split_axis=2, concat_axis=0, tiled=True)  23.1 us
    unnamed x1, other arithmetic  22.4 us
    unnamed x21, local copies, waits for them, and re-layouts  7.27 us
  transfers between devices with their start and end apart: 4, of which 4 were waited for; matrix products, arithmetic and copies ran while one was open for 8% of the time, Pallas kernels for 0%

profile of v1, /device:TPU:1, one launch (start us, length us, event | category | flops | bytes accessed | tf_op | source)
XLA Modules:
  0.0 347.4 jit_solution(17336180844059140672)
XLA Ops:
  7.2 0.0 all-gather.3.cloned.1.call-start
  7.2 1.8 reshape_squeeze.16
  9.0 0.0 copy-start.5
  9.0 0.0 copy-start
  9.0 0.0 copy-start.1
  9.0 2.0 reshape_squeeze.17
  11.0 2.3 pad_maximum_fusion
  13.3 1.2 reshape.51
  14.5 0.0 all-gather.3.cloned.1.call-update
  14.5 0.0 reduce-scatter.5.cloned.1.call-start
  14.5 0.0 copy-done.5
  14.6 0.2 reduce-window.9
  14.7 0.1 pad_add_fusion.info
  14.8 59.9 %all-gather.3.cloned.1.call-done.kv_ref = bf16[2048,2048]{1,0:T(8,128)(2,1)} async-done(((bf16[128,2048]{1,0:T(8,128)(2,1)}), bf16[2048,2048]{1,0:T(8,128)(2,1)}) %all-gather.3.cloned.1.call-update) | async-done | bytes 8388624 | tf_op jit(solution)/shard_map/all_gather | solution.py:182
  74.7 0.0 copy-done
  74.7 0.0 copy-done.1
  74.7 26.8 %attention_grads.1 = (bf16[128,5120]{1,0:T(8,128)(2,1)}, bf16[2048,2048]{1,0:T(8,128)(2,1)}) custom-call(s32[17]{0:T(128)S(1)} %pad_add_fusion.info, bf16[128,5120]{1,0:T(8,128)(2,1)S(1)} %bitcast.22, bf16[128,5120]{1,0:T(8,128)(2,1)S(1)} %bitcast.23, bf16[2048,2048]{1,0:T(8,128)(2,1)} %all-gather.3.cloned.1.call-done.kv_ref), custom_call_target="tpu_custom_call" | custom-call | flops 13421772800 | bytes 31457280 | tf_op jit(solution)/shard_map/attention_grads/pallas_call | solution.py:142
  101.4 0.0 reduce-scatter.5.cloned.1.call-update
  101.5 0.0 copy-start.4
  101.5 0.0 all-gather.5.cloned.1.call-start
  101.5 121.8 %reduce-scatter.5.cloned.1.call-done = bf16[128,2048]{1,0:T(8,128)(2,1)} async-done(((bf16[2048,2048]{1,0:T(8,128)(2,1)}), bf16[128,2048]{1,0:T(8,128)(2,1)}) %reduce-scatter.5.cloned.1.call-update) | async-done | bytes 524304 | tf_op jit(solution)/shard_map/reduce_scatter | solution.py:188
  223.4 1.4 reshape.52
  224.8 0.0 copy-start.2
  224.8 0.3 slice.9
  225.1 0.2 copy.40
  225.2 0.8 copy.31
  226.0 0.0 all-gather.5.cloned.1.call-update
  226.0 0.0 copy-done.2
  226.0 0.0 reduce-scatter.7.cloned.1.call-start
  226.1 0.0 copy-done.4
  226.1 2.8 copy.32
  228.9 0.5 broadcast
  229.5 22.4 %reduce = bf16[4096,128]{1,0:T(8,128)(2,1)S(1)} reduce(bf16[4096,1,128]{2,1,0:T(2,128)(2,1)S(1)} %bitcast.25, bf16[]{:T(256)} %broadcast), dimensions={1}, to_apply=%bitcast.17.reduce_sub_computation | reduce | bytes 2097154
  251.9 0.3 reshape.57
  252.1 23.1 %all_to_all.15 = bf16[16,2,16384]{2,1,0:T(2,128)(2,1)S(1)} all-to-all(bf16[16,2,16384]{2,1,0:T(2,128)(2,1)S(1)} %reshape.57), channel_id=1, replica_groups=mesh['dp'=16,'seq'=16] {'dp'}, dimensions={0} | all-to-all | bytes 2097152 | tf_op jit(solution)/shard_map/all_to_all | solution.py:176
  275.2 1.0 reshape.58
  276.3 0.1 copy.38
  276.4 0.5 copy.33
  277.0 6.8 %all-gather.5.cloned.1.call-done = bf16[16,128,512]{2,1,0:T(8,128)(2,1)} async-done(((bf16[1,128,512]{2,1,0:T(8,128)(2,1)}), bf16[16,128,512]{2,1,0:T(8,128)(2,1)}) %all-gather.5.cloned.1.call-update) | async-done | bytes 2097168 | tf_op jit(solution)/shard_map/all_gather | solution.py:192
  283.7 0.0 copy-start.3
  283.7 2.4 convolution_bitcast_fusion
  286.1 1.0 copy.36
  287.1 0.0 reduce-scatter.7.cloned.1.call-update
  287.1 0.0 copy-done.3
  287.1 0.4 copy.39
  287.6 0.9 copy.34
  288.4 52.4 %reduce-scatter.7.cloned.1.call-done = f32[16,512]{1,0:T(8,128)} async-done(((f32[256,512]{1,0:T(8,128)}), f32[16,512]{1,0:T(8,128)}) %reduce-scatter.7.cloned.1.call-update) | async-done | bytes 32784
  (1 shorter events, 0.0 us)
Async XLA Ops:
  7.2 67.5 %all-gather.3.cloned.1.call-start = ((), (), s32[]{:S(2)}) async-start(), calls=%async_computation.3 | async-start | bytes 8912896 | tf_op jit(solution)/shard_map/all_gather | solution.py:182
  9.0 5.5 %copy-start.5 = (s32[8]{0:T(128)S(1)}, s32[8]{0:T(128)}, u32[]{:S(2)}) copy-start(s32[8]{0:T(128)} %param.11) | copy-start | bytes 100
  9.0 65.7 %copy-start = (bf16[1,128,5120]{2,1,0:T(8,128)(2,1)S(1)}, bf16[1,128,5120]{2,1,0:T(8,128)(2,1)}, u32[]{:S(2)}) copy-start(bf16[1,128,5120]{2,1,0:T(8,128)(2,1)} %param.6) | copy-start | bytes 3932164
  9.0 65.7 %copy-start.1 = (bf16[1,128,5120]{2,1,0:T(8,128)(2,1)S(1)}, bf16[1,128,5120]{2,1,0:T(8,128)(2,1)}, u32[]{:S(2)}) copy-start(bf16[1,128,5120]{2,1,0:T(8,128)(2,1)} %param.9) | copy-start | bytes 3932164
  14.5 208.9 %reduce-scatter.5.cloned.1.call-start = ((), (), s32[]{:S(2)}) async-start(), calls=%async_computation.4 | async-start | bytes 8912896 | tf_op jit(solution)/shard_map/reduce_scatter | solution.py:188
  101.5 124.6 %copy-start.4 = (bf16[1,128,4096]{2,1,0:T(8,128)(2,1)S(1)}, bf16[1,128,4096]{2,1,0:T(8,128)(2,1)}, u32[]{:S(2)}) copy-start(bf16[1,128,4096]{2,1,0:T(8,128)(2,1)} %param.10) | copy-start | bytes 3145732
  101.5 182.2 %all-gather.5.cloned.1.call-start = ((), (), s32[]{:S(2)}) async-start(), calls=%async_computation.5 | async-start | bytes 2228224 | tf_op jit(solution)/shard_map/all_gather | solution.py:192
  224.8 1.3 copy-start.2
  226.0 114.8 %reduce-scatter.7.cloned.1.call-start = ((), (), s32[]{:S(2)}) async-start(), calls=%async_computation.6 | async-start | bytes 557056
  283.7 3.4 copy-start.3
Sparse Core Ops, SparseCore 0:
  14.6 60.0 all-gather.2
  101.6 121.7 reduce-scatter.4
  226.4 57.2 all-gather.4
  287.3 53.5 reduce-scatter.6

commit v2 on v1

--- a/solution.py
+++ b/solution.py
@@ -28,11 +28,323 @@
     return op(x.reshape(rows // 8, 8, columns), axis=0)
 
 
+MESH = pl.DeviceIdType.MESH
+
+
+def barrier_with(peers):
+    barrier = pltpu.get_barrier_semaphore()
+    for peer in peers:
+        pl.semaphore_signal(barrier, inc=1, device_id=peer, device_id_type=MESH)
+    pl.semaphore_wait(barrier, len(peers))
+
+
+class Sender:
+    def __init__(self, send_sems, recv_sems):
+        self.send_sems, self.recv_sems, self.used = send_sems, recv_sems, 0
+
+    def start(self, source, target, peer):
+        copy = pltpu.make_async_remote_copy(
+            src_ref=source,
+            dst_ref=target,
+            send_sem=self.send_sems.at[self.used],
+            recv_sem=self.recv_sems.at[self.used],
+            device_id=peer,
+            device_id_type=MESH,
+        )
+        self.used += 1
+        copy.start()
+        return copy
+
+
+def places():
+    dp = lax.axis_index("dp")
+    seq = lax.axis_index("seq")
+    dps = lax.axis_size("dp")
+    chips = lax.axis_size("seq") // 2
+    z = seq // 2
+    core = lax.rem(seq, 2)
+    partner = (dp, 2 * z + 1 - core)
+
+    def chip(offset):
+        return (dp, 2 * lax.rem(z + offset + chips, chips) + core)
+
+    def row(offset):
+        return (lax.rem(dp + offset, dps), seq)
+
+    return dp, seq, dps, chips, z, core, partner, chip, row
+
+
+def gather_kernel(k_ref, v_ref, x_ref, kv_out, x_out, sends, recvs, local_sems):
+    dp, seq, dps, chips, z, core, partner, chip, row = places()
+    half = chips // 2
+    width = k_ref.shape[1]
+    parts = x_out.shape[2]
+    barrier_with(
+        [chip(1), chip(-1), partner] + [row(k) for k in range(1, dps)]
+    )
+    sender = Sender(sends, recvs)
+    mine = kv_out.at[seq]
+    key_part, value_part = pl.ds(0, width), pl.ds(width, width)
+    first = {}
+    for way in (1, -1):
+        first[way] = [
+            sender.start(k_ref, mine.at[:, key_part], chip(way)),
+            sender.start(v_ref, mine.at[:, value_part], chip(way)),
+        ]
+    passed = [
+        sender.start(k_ref, mine.at[:, key_part], partner),
+        sender.start(v_ref, mine.at[:, value_part], partner),
+    ]
+    locals_ = [
+        pltpu.make_async_copy(k_ref, mine.at[:, key_part], local_sems.at[0]),
+        pltpu.make_async_copy(v_ref, mine.at[:, value_part], local_sems.at[1]),
+        pltpu.make_async_copy(
+            x_ref.at[:, pl.ds(pl.multiple_of(dp * parts, parts), parts)],
+            x_out.at[dp], local_sems.at[2],
+        ),
+    ]
+    for copy in locals_:
+        copy.start()
+    exchanged = []
+    for k in range(1, dps):
+        target = lax.rem(dp + k, dps)
+        exchanged.append(
+            sender.start(
+                x_ref.at[:, pl.ds(pl.multiple_of(target * parts, parts), parts)],
+                x_out.at[dp], row(k),
+            )
+        )
+    waiting = dict(first)
+    sent = []
+    for step in range(1, half + 1):
+        for way in (1, -1):
+            for copy in waiting[way]:
+                copy.wait_recv()
+            sent += waiting[way]
+            slot = 2 * lax.rem(z - way * step + chips, chips) + core
+            block = kv_out.at[slot]
+            if step == half:
+                part = pl.ds(0 if way == 1 else width, width)
+                block = block.at[:, part]
+                passed.append(sender.start(block, block, partner))
+                continue
+            onward = block
+            if step == half - 1:
+                part = pl.ds(0 if way == 1 else width, width)
+                onward = block.at[:, part]
+            waiting[way] = [sender.start(onward, onward, chip(way))]
+            passed.append(sender.start(block, block, partner))
+    for copy in locals_:
+        copy.wait()
+    for copy in passed + exchanged:
+        copy.wait_recv()
+    for copy in sent + passed + exchanged:
+        copy.wait_send()
+
+
+def gather_exchange(keys, values, layer_input, first_columns):
+    tokens = keys.shape[0]
+    dps = lax.axis_size("dp")
+    members = lax.axis_size("seq")
+    chips = members // 2
+    width = VGW * HD
+    parts = layer_input.shape[1] // dps
+    copies = 4 + 2 + (dps - 1) + 2 * (chips // 2 - 1) + 2 * (chips // 2)
+    column = pl.BlockSpec((tokens, width), lambda i: (0, 0))
+    return pl.pallas_call(
+        gather_kernel,
+        out_shape=(
+            jax.ShapeDtypeStruct((members, tokens, 2 * width), jnp.bfloat16),
+            jax.ShapeDtypeStruct((dps, tokens, parts), jnp.bfloat16),
+        ),
+        grid=(1,),
+        in_specs=[column, column, pl.BlockSpec(memory_space=pltpu.VMEM)],
+        out_specs=(pl.BlockSpec(memory_space=pl.ANY), pl.BlockSpec(memory_space=pl.ANY)),
+        scratch_shapes=[
+            pltpu.SemaphoreType.DMA((copies,)),
+            pltpu.SemaphoreType.DMA((copies,)),
+            pltpu.SemaphoreType.DMA((3,)),
+        ],
+        compiler_params=pltpu.CompilerParams(collective_id=0, has_side_effects=True),
+        name="gather_exchange",
+    )(keys, values, layer_input)
+
+
+def reduce_kernel(
+    dk_ref, v_ref, x_ref, dk_out, w_out,
+    pair_k, ring_in, ring_out, fin_out, fin_in,
+    v_all, w_part, w_pair, w_sum, w_in, w_fin, w_fin_in,
+    sends, recvs, local_sem,
+):
+    dp, seq, dps, chips, z, core, partner, chip, row = places()
+    tokens = v_ref.shape[0]
+    half = dk_ref.shape[2] // 2
+    quarter = half // 2
+    whalf = w_part.shape[2] // 2
+    other = 1 - core
+    barrier_with(
+        [partner]
+        + [chip(k) for k in range(1, chips)]
+        + [row(k) for k in range(1, dps)]
+    )
+    sender = Sender(sends, recvs)
+
+    def at_chip(offset):
+        return lax.rem(z + offset + 2 * chips, chips)
+
+    order = []
+    for k in range(1, chips // 2):
+        order += [-k, k]
+    order += [chips // 2, 0]
+    index_of = {offset % chips: i for i, offset in enumerate(order)}
+    mine_columns = pl.multiple_of(core * half, half)
+    other_columns = pl.multiple_of(other * half, half)
+    paired = [
+        sender.start(
+            dk_ref.at[at_chip(offset), :, pl.ds(other_columns, half)],
+            pair_k.at[i], partner,
+        )
+        for i, offset in enumerate(order)
+    ]
+    own_v = pltpu.make_async_copy(v_ref, v_all.at[dp], local_sem.at[0])
+    own_v.start()
+    spread = [sender.start(v_ref, v_all.at[dp], row(k)) for k in range(1, dps)]
+
+    arrived = set()
+
+    def own_sum(offset, way_index, rows):
+        i = index_of[offset % chips]
+        if i not in arrived:
+            paired[i].wait_recv()
+            arrived.add(i)
+        start = pl.multiple_of(mine_columns + way_index * quarter, quarter)
+        mine = dk_ref[at_chip(offset), rows, pl.ds(start, quarter)]
+        theirs = pair_k[i, rows, way_index * quarter:(way_index + 1) * quarter]
+        return mine.astype(jnp.float32) + theirs.astype(jnp.float32)
+
+    flights = {}
+    sent = []
+    for step in range(chips):
+        for part in range(2):
+            rows = slice(part * tokens, (part + 1) * tokens)
+            for way_index, way in enumerate((1, -1)):
+                value = own_sum(-way * (1 + step), way_index, rows)
+                if step:
+                    copy = flights[part, way]
+                    copy.wait_recv()
+                    sent.append(copy)
+                    value = value + ring_in[way_index, part, step - 1].astype(jnp.float32)
+                value = value.astype(jnp.bfloat16)
+                if step < chips - 1:
+                    ring_out[way_index, part, step] = value
+                    flights[part, way] = sender.start(
+                        ring_out.at[way_index, part, step],
+                        ring_in.at[way_index, part, step],
+                        chip(way),
+                    )
+                else:
+                    fin_out[part, :, way_index * quarter:(way_index + 1) * quarter] = value
+    back = sender.start(fin_out.at[other], fin_in, partner)
+    dk_out[:, pl.ds(mine_columns, half)] = fin_out[core]
+
+    own_v.wait()
+    for copy in spread:
+        copy.wait_recv()
+    parts = x_ref.shape[2]
+    joined = min(4, dps)
+
+    def multiply(i, total):
+        window = pl.ds(i * joined, joined)
+        return total + lax.dot_general(
+            x_ref[window].reshape(joined * tokens, parts),
+            v_all[window].reshape(joined * tokens, v_ref.shape[1]),
+            (((0,), (0,)), ((), ())),
+            preferred_element_type=jnp.float32,
+        )
+
+    total = lax.fori_loop(
+        0, dps // joined, multiply, jnp.zeros((parts, v_ref.shape[1]), jnp.float32)
+    )
+    w_part[...] = total.reshape(w_part.shape)
+    w_mine = pl.multiple_of(core * whalf, whalf)
+    w_other = pl.multiple_of(other * whalf, whalf)
+    w_paired = sender.start(w_part.at[:, :, pl.ds(w_other, whalf)], w_pair, partner)
+    back.wait_recv()
+    dk_out[:, pl.ds(other_columns, half)] = fin_in[...]
+    w_paired.wait_recv()
+    w_sum[...] = w_part[:, :, pl.ds(w_mine, whalf)] + w_pair[...]
+    direct = [
+        sender.start(w_sum.at[at_chip(k)], w_in.at[k - 1], chip(k)) for k in range(1, chips)
+    ]
+    total = w_sum[z]
+    for k, copy in enumerate(direct):
+        copy.wait_recv()
+        total = total + w_in[k]
+    owned = w_out.shape[0]
+    w_fin[...] = total.reshape(w_fin.shape)
+    w_back = sender.start(w_fin.at[other], w_fin_in, partner)
+    w_out[:, pl.ds(w_mine, whalf)] = w_fin[core]
+    w_back.wait_recv()
+    w_out[:, pl.ds(w_other, whalf)] = w_fin_in[...]
+    for copy in paired + spread + sent + [back, w_paired, w_back] + direct:
+        copy.wait_send()
+
+
+def reduce_exchange(dk, value_window, input_parts):
+    tokens, vwidth = value_window.shape
+    dps = lax.axis_size("dp")
+    members = lax.axis_size("seq")
+    chips = members // 2
+    kwidth = dk.shape[1]
+    parts = input_parts.shape[2]
+    owned = parts // members
+    copies = chips + (dps - 1) + 4 * (chips - 1) + 3 + (chips - 1)
+    vmem = pl.BlockSpec(memory_space=pltpu.VMEM)
+    bf, f32 = jnp.bfloat16, jnp.float32
+    return pl.pallas_call(
+        reduce_kernel,
+        out_shape=(
+            jax.ShapeDtypeStruct((tokens, kwidth), bf),
+            jax.ShapeDtypeStruct((owned, vwidth), f32),
+        ),
+        in_specs=[vmem] * 3,
+        out_specs=(vmem, vmem),
+        scratch_shapes=[
+            pltpu.VMEM((chips, 2 * tokens, kwidth // 2), bf),
+            pltpu.VMEM((2, 2, chips - 1, tokens, kwidth // 4), bf),
+            pltpu.VMEM((2, 2, chips - 1, tokens, kwidth // 4), bf),
+            pltpu.VMEM((2, tokens, kwidth // 2), bf),
+            pltpu.VMEM((tokens, kwidth // 2), bf),
+            pltpu.VMEM((dps, tokens, vwidth), bf),
+            pltpu.VMEM((chips, 2 * owned, vwidth), f32),
+            pltpu.VMEM((chips, 2 * owned, vwidth // 2), f32),
+            pltpu.VMEM((chips, 2 * owned, vwidth // 2), f32),
+            pltpu.VMEM((chips - 1, 2 * owned, vwidth // 2), f32),
+            pltpu.VMEM((2, owned, vwidth // 2), f32),
+            pltpu.VMEM((owned, vwidth // 2), f32),
+            pltpu.SemaphoreType.DMA((copies,)),
+            pltpu.SemaphoreType.DMA((copies,)),
+            pltpu.SemaphoreType.DMA((1,)),
+        ],
+        compiler_params=pltpu.CompilerParams(
+            collective_id=1, has_side_effects=True, vmem_limit_bytes=48 * 1024 * 1024
+        ),
+        name="reduce_exchange",
+    )(dk.reshape(chips, 2 * tokens, kwidth), value_window, input_parts)
+
+
 def attention_kernel(
-    info, q_ref, do_ref, kv_ref, dq_ref, dkv_ref,
-    qs, dos, s_scr, dp_scr, acc, kt_scr,
+    base, with_value, info, q_ref, do_ref, k_ref, v_ref, *refs
 ):
-    group = pl.program_id(0)
+    if base:
+        dq_before, *refs = refs
+    dq_ref, dkv_ref, qs, dos, s_scr, dp_scr, acc, kt_scr = refs
+    if base:
+        @pl.when(pl.program_id(0) == 0)
+        def _():
+            dq_ref[...] = dq_before[...]
+
+    group = base + pl.program_id(0)
     block = info[2 * KVG]
     first_head = info[group]
     head_count = info[KVG + group]
@@ -47,8 +359,8 @@
 
     def prepare(c, _):
         rows = rows_at(c)
-        kt_scr[:, rows] = kv_ref[rows, :HD].T
-        acc[rows, :] = jnp.zeros((CHUNK, 2 * HD), jnp.float32)
+        kt_scr[:, rows] = k_ref[rows, :].T
+        acc[rows, :] = jnp.zeros((CHUNK, acc.shape[1]), jnp.float32)
         return 0
 
     lax.fori_loop(0, last + 1, prepare, 0)
@@ -64,7 +376,7 @@
 
         def scores(c, top, masked):
             rows = rows_at(c)
-            s = matmul(kv_ref[rows, :HD], q, NT)
+            s = matmul(k_ref[rows, :], q, NT)
             if masked:
                 key_at = c * CHUNK + lax.broadcasted_iota(jnp.int32, (CHUNK, width), 0)
                 row_at = row_base + lax.rem(
@@ -85,7 +397,7 @@
             total, term = carry
             rows = rows_at(c)
             e = jnp.exp2(s_scr[rows, :width] * to_exp2 - shift)
-            dp = matmul(kv_ref[rows, HD:], do, NT)
+            dp = matmul(v_ref[rows, :], do, NT)
             s_scr[rows, :width] = e
             dp_scr[rows, :width] = dp
             return (total + fold_rows(e, jnp.sum), term + fold_rows(e * dp, jnp.sum))
@@ -99,7 +411,8 @@
             rows = rows_at(c)
             p = s_scr[rows, :width] * inverse
             ds = (p * (dp_scr[rows, :width] - row_term)).astype(jnp.bfloat16)
-            acc[rows, HD:] += matmul(p.astype(jnp.bfloat16), do, NN)
+            if with_value:
+                acc[rows, HD:] += matmul(p.astype(jnp.bfloat16), do, NN)
             acc[rows, :HD] += matmul(ds, q, NN)
             return dqt + matmul(kt_scr[:, rows], ds, NN)
 
@@ -122,40 +435,45 @@
     def finish(c, _):
         rows = rows_at(c)
         dkv_ref[rows, :HD] = (acc[rows, :HD] * scaling).astype(dkv_ref.dtype)
-        dkv_ref[rows, HD:] = acc[rows, HD:].astype(dkv_ref.dtype)
+        if with_value:
+            dkv_ref[rows, HD:] = acc[rows, HD:].astype(dkv_ref.dtype)
         return 0
 
     lax.fori_loop(0, last + 1, finish, 0)
 
     def clear(c, _):
-        dkv_ref[rows_at(c), :] = jnp.zeros((CHUNK, 2 * HD), dkv_ref.dtype)
+        dkv_ref[rows_at(c), :] = jnp.zeros((CHUNK, dkv_ref.shape[1]), dkv_ref.dtype)
         return 0
 
     lax.fori_loop(last + 1, dkv_ref.shape[0] // CHUNK, clear, 0)
 
 
-def attention_grads(queries, grads, kv, info):
+def attention_grads(queries, grads, kv, info, base, with_value, before=None):
     tokens, width = queries.shape
-    sequence = kv.shape[0]
+    sequence, kv_width = kv.shape
+    groups = kv_width // (2 * HD)
+    wide = 2 * HD if with_value else HD
     whole = pl.BlockSpec((tokens, width), lambda g, info: (0, 0))
-    group_block = pl.BlockSpec((sequence, 2 * HD), lambda g, info: (0, g))
+    key_block = pl.BlockSpec((sequence, HD), lambda g, info: (0, g))
+    value_block = pl.BlockSpec((sequence, HD), lambda g, info: (0, groups + g))
+    given = () if before is None else (before,)
     return pl.pallas_call(
-        attention_kernel,
+        functools.partial(attention_kernel, base, with_value),
         out_shape=(
             jax.ShapeDtypeStruct((tokens, width), jnp.bfloat16),
-            jax.ShapeDtypeStruct(kv.shape, jnp.bfloat16),
+            jax.ShapeDtypeStruct((sequence, groups * wide), jnp.bfloat16),
         ),
         grid_spec=pltpu.PrefetchScalarGridSpec(
             num_scalar_prefetch=1,
-            grid=(KVG,),
-            in_specs=[whole, whole, group_block],
-            out_specs=[whole, group_block],
+            grid=(groups,),
+            in_specs=[whole, whole, key_block, value_block] + [whole] * len(given),
+            out_specs=[whole, pl.BlockSpec((sequence, wide), lambda g, info: (0, g))],
             scratch_shapes=[
                 pltpu.VMEM((2 * tokens, HD), jnp.bfloat16),
                 pltpu.VMEM((2 * tokens, HD), jnp.bfloat16),
                 pltpu.VMEM((sequence, 2 * tokens), jnp.float32),
                 pltpu.VMEM((sequence, 2 * tokens), jnp.float32),
-                pltpu.VMEM((sequence, 2 * HD), jnp.float32),
+                pltpu.VMEM((sequence, wide), jnp.float32),
                 pltpu.VMEM((HD, sequence), jnp.bfloat16),
             ],
         ),
@@ -168,36 +486,33 @@
             transcendentals=HKEPT * tokens * sequence,
         ),
         name="attention_grads",
-    )(info, queries, grads, kv)
+    )(info, queries, grads, kv, kv, *given)
 
 
 def local(query_states, key_states, value_states, output_grad, layer_input, head_counts):
     tokens = query_states.shape[1]
-    input_parts = lax.all_to_all(
-        layer_input, "dp", split_axis=2, concat_axis=0, tiled=True
-    )
-    keys = key_states[0].reshape(tokens, KVG, 1, HD)
-    values = value_states[0].reshape(tokens, KVG, 1, HD)
-    kv_local = jnp.concatenate([keys, values], axis=2).reshape(tokens, 2 * KVG * HD)
-    kv = lax.all_gather(kv_local, "seq", axis=0, tiled=True)
+    keys, values, queries, grads = key_states[0], value_states[0], query_states[0], output_grad[0]
+    split = VGW * HD
     group_ends = jnp.cumsum(head_counts)
     info = jnp.concatenate(
         [group_ends - head_counts, head_counts, lax.axis_index("seq").reshape(1)]
     ).astype(jnp.int32)
-    query_grad, dkv = attention_grads(query_states[0], output_grad[0], kv, info)
-    summed = lax.psum_scatter(dkv, "seq", scatter_dimension=0, tiled=True)
-    summed = summed.reshape(tokens, KVG, 2, HD)
-    key_grad = summed[:, :, 0, :].reshape(1, tokens, KVG * HD)
-    value_window = summed[:, :VGW, 1, :].reshape(1, tokens, VGW * HD)
-    value_all = lax.all_gather(value_window, "dp", axis=0, tiled=True)
-    weight_part = lax.dot_general(
-        input_parts.reshape(-1, input_parts.shape[2]),
-        value_all.reshape(-1, VGW * HD),
-        (((0,), (0,)), ((), ())),
-        preferred_element_type=jnp.float32,
+    kv_late = jnp.concatenate([keys[:, split:], values[:, split:]], axis=1)
+    kv_first, input_parts = gather_exchange(keys, values, layer_input[0], split)
+    kv_first, kv_late = lax.optimization_barrier((kv_first, kv_late))
+    kv_first = kv_first.reshape(-1, 2 * split)
+    kv_late = lax.all_gather(kv_late, "seq", axis=0, tiled=True)
+    query_grad, dkv_first = attention_grads(queries, grads, kv_first, info, 0, True)
+    query_grad, dk_late = attention_grads(
+        queries, grads, kv_late, info, VGW, False, query_grad
     )
-    weight_grad = lax.psum_scatter(weight_part, "seq", scatter_dimension=0, tiled=True)
-    return (query_grad[None], key_grad, weight_grad)
+    summed = lax.psum_scatter(dkv_first, "seq", scatter_dimension=0, tiled=True)
+    summed = summed.reshape(tokens, VGW, 2, HD)
+    key_first = summed[:, :, 0, :].reshape(tokens, split)
+    value_window = summed[:, :, 1, :].reshape(tokens, split)
+    key_late, weight_grad = reduce_exchange(dk_late, value_window, input_parts)
+    key_grad = jnp.concatenate([key_first, key_late], axis=1)
+    return (query_grad[None], key_grad[None], weight_grad)
 
 
 def solution(mesh):

time: 350 us -> 212 us (0.61)
  waiting for transfers between devices: 241 us -> 65 us
  Pallas kernels: 26.8 us -> 122 us
  other arithmetic: 24.9 us -> 1.73 us
  blocking collectives: 23.1 us -> 0 us
  local copies, waits for them, and re-layouts: 15.2 us -> 8.93 us
    pallas_call x1 -> x4, Pallas kernels: 26.8 us -> 122 us  [the longest x1 52.9 us: reduce_exchange(): pl.pallas_call(reduce_kernel, out_shape=(jax.ShapeDtypeStruct((tokens, kw...]
    reduce_scatter x1, waiting for transfers between devices: 122 us -> 40.9 us  [local(): summed = lax.psum_scatter(dkv_first, 'seq', scatter_dimension=0, tiled=True)]
    unnamed x5 -> x2, waiting for transfers between devices: 52.5 us -> 0.03 us
    all_gather x2 -> x1, waiting for transfers between devices: 66.6 us -> 24.1 us  [local(): kv_late = lax.all_gather(kv_late, 'seq', axis=0, tiled=True)]
    all_to_all x1 -> x0, blocking collectives: 23.1 us -> none  [local(): lax.all_to_all(layer_input, 'dp', split_axis=2, concat_axis=0, tiled=True)]
    unnamed x1 -> x0, other arithmetic: 22.4 us -> none
    another operation x3 -> x0, local copies, waits for them, and re-layouts: 4.55 us -> none  [the longest x1 1.96 us: local(): values = value_states[0].reshape(tokens, KVG, 1, HD)]
    unnamed x21 -> x17, local copies, waits for them, and re-layouts: 7.27 us -> 4.36 us
  transfers between devices with their start and end apart: 4 -> 2, of which waited for: 4 -> 2; matrix products, arithmetic and copies ran while one was open for 8% -> 0% of each run, Pallas kernels for 0% -> 13%
where the time goes in v2:
time: 212 us
  Pallas kernels  122 us (58%)
  waiting for transfers between devices  65 us (31%)
  between operations  14.1 us (7%)
  local copies, waits for them, and re-layouts  8.93 us (4%)
    pallas_call x1, Pallas kernels, reduce_exchange(): pl.pallas_call(reduce_kernel, out_shape=(jax.ShapeDtypeStruct((tokens, kw...  52.9 us
    reduce_scatter x1, waiting for transfers between devices, local(): summed = lax.psum_scatter(dkv_first, 'seq', scatter_dimension=0, tiled=True)  40.9 us
    pallas_call x1, Pallas kernels, gather_exchange(): pl.pallas_call(gather_kernel, out_shape=(jax.ShapeDtypeStruct((members, t...  40.5 us
    pallas_call x2, Pallas kernels, attention_grads(): pl.pallas_call(functools.partial(attention_kernel, base, with_value), out...  28.3 us
    all_gather x1, waiting for transfers between devices, local(): kv_late = lax.all_gather(kv_late, 'seq', axis=0, tiled=True)  24.1 us
    unnamed x17, local copies, waits for them, and re-layouts  4.36 us
  transfers between devices with their start and end apart: 2, of which 2 were waited for; matrix products, arithmetic and copies ran while one was open for 0% of the time, Pallas kernels for 13%

profile of v2, /device:TPU:1, one launch (start us, length us, event | category | flops | bytes accessed | tf_op | source)
XLA Modules:
  0.0 211.6 jit_solution(9318965656539092775)
XLA Ops:
  7.2 0.0 copy-start.6
  7.2 0.0 copy-start.1
  7.2 0.0 copy-start.2
  7.2 0.0 all-gather.2.cloned.1.call-start
  7.2 1.1 slice.16
  8.3 0.9 slice.17
  9.2 40.5 %gather_exchange.1 = (bf16[16,128,1024]{2,1,0:T(8,128)(2,1)}, bf16[16,128,256]{2,1,0:T(8,128)(2,1)}) custom-call(bf16[128,1024]{1,0:T(8,128)(2,1)} %bitcast.32, bf16[128,1024]{1,0:T(8,128)(2,1)} %bitcast.30, bf16[128,4096]{1,0:T(8,128)(2,1)} %bitcast.28), custom_call_target="tpu_custom_call" | custom-call | tf_op jit(solution)/shard_map/gather_exchange/pallas_call | solution.py:154
  49.8 0.7 pad_maximum_fusion
  50.5 0.0 all-gather.2.cloned.1.call-update
  50.5 0.0 reduce-scatter.2.cloned.1.call-start
  50.6 0.0 copy-done.6
  50.6 0.2 reduce-window.9
  50.8 0.1 pad_add_fusion.info
  50.9 0.0 copy-done.1
  50.9 0.0 copy-done.2
  50.9 11.0 %attention_grads.2 = (bf16[128,5120]{1,0:T(8,128)(2,1)S(1)}, bf16[2048,1024]{1,0:T(8,128)(2,1)}) custom-call(s32[17]{0:T(128)S(1)} %pad_add_fusion.info, bf16[128,5120]{1,0:T(8,128)(2,1)S(1)} %bitcast.24, bf16[128,5120]{1,0:T(8,128)(2,1)S(1)} %bitcast.26, bf16[2048,1024]{1,0:T(8,128)(2,1)} %bitcast.37, bf16[2048,1024]{1,0:T(8,128)(2,1)} %bitcast.38), custom_call_target="tpu_custom_call" | custom-call | flops 13421772800 | bytes 31457280 | tf_op jit(solution)/shard_map/attention_grads/pallas_call | solution.py:460
  61.9 0.0 copy-start.4
  61.9 1.1 copy-done.4
  63.0 0.0 reduce-scatter.2.cloned.1.call-update
  63.0 24.1 %all-gather.2.cloned.1.call-done.k_ref.v_ref = bf16[2048,1024]{1,0:T(8,128)(2,1)} async-done(((bf16[128,1024]{1,0:T(8,128)(2,1)}), bf16[2048,1024]{1,0:T(8,128)(2,1)}) %all-gather.2.cloned.1.call-update) | async-done | bytes 4194320 | tf_op jit(solution)/shard_map/all_gather | solution.py:504
  87.1 0.0 copy-start.3
  87.1 1.3 copy-done.3
  88.4 0.0 copy-start.5
  88.4 1.3 copy-done.5
  89.7 17.3 %attention_grads.3 = (bf16[128,5120]{1,0:T(8,128)(2,1)}, bf16[2048,512]{1,0:T(8,128)(2,1)S(1)}) custom-call(s32[17]{0:T(128)S(1)} %pad_add_fusion.info, bf16[128,5120]{1,0:T(8,128)(2,1)S(1)} %bitcast.25, bf16[128,5120]{1,0:T(8,128)(2,1)S(1)} %bitcast.27, bf16[2048,1024]{1,0:T(8,128)(2,1)} %all-gather.2.cloned.1.call-done.k_ref.v_ref, ...), custom_call_target="tpu_custom_call" | custom-call | flops 13421772800 | bytes 31457280 | tf_op jit(solution)/shard_map/attention_grads/pallas_call | solution.py:460
  107.0 0.0 copy-start
  107.0 40.9 %reduce-scatter.2.cloned.1.call-done = bf16[128,1024]{1,0:T(8,128)(2,1)} async-done(((bf16[2048,1024]{1,0:T(8,128)(2,1)}), bf16[128,1024]{1,0:T(8,128)(2,1)}) %reduce-scatter.2.cloned.1.call-update) | async-done | bytes 262160 | tf_op jit(solution)/shard_map/reduce_scatter | solution.py:509
  147.8 1.1 reshape.48
  149.0 1.5 slice_reduce_fusion.1
  150.5 0.0 copy-done
  150.5 52.9 %reduce_exchange.1 = (bf16[128,512]{1,0:T(8,128)(2,1)S(1)}, f32[16,512]{1,0:T(8,128)S(1)}) custom-call(bf16[8,256,512]{2,1,0:T(8,128)(2,1)S(1)} %bitcast.22, bf16[128,512]{1,0:T(8,128)(2,1)S(1)} %bitcast.23, bf16[16,128,256]{2,1,0:T(8,128)(2,1)S(1)} %copy-done), custom_call_target="tpu_custom_call" | custom-call | tf_op jit(solution)/shard_map/reduce_exchange/pallas_call | solution.py:304
  203.4 0.7 maximum_bitcast_fusion
  204.1 0.6 copy.20
  (3 shorter events, 0.0 us)
Async XLA Ops:
  7.2 43.4 %copy-start.6 = (s32[8]{0:T(128)S(1)}, s32[8]{0:T(128)}, u32[]{:S(2)}) copy-start(s32[8]{0:T(128)} %param.11) | copy-start | bytes 100
  7.2 43.7 %copy-start.1 = (bf16[1,128,5120]{2,1,0:T(8,128)(2,1)S(1)}, bf16[1,128,5120]{2,1,0:T(8,128)(2,1)}, u32[]{:S(2)}) copy-start(bf16[1,128,5120]{2,1,0:T(8,128)(2,1)} %param.6) | copy-start | bytes 3932164
  7.2 43.7 %copy-start.2 = (bf16[1,128,5120]{2,1,0:T(8,128)(2,1)S(1)}, bf16[1,128,5120]{2,1,0:T(8,128)(2,1)}, u32[]{:S(2)}) copy-start(bf16[1,128,5120]{2,1,0:T(8,128)(2,1)} %param.9) | copy-start | bytes 3932164
  7.2 79.9 %all-gather.2.cloned.1.call-start = ((), (), s32[]{:S(2)}) async-start(), calls=%async_computation.1 | async-start | bytes 4456448 | tf_op jit(solution)/shard_map/all_gather | solution.py:504
  50.5 97.3 %reduce-scatter.2.cloned.1.call-start = ((), (), s32[]{:S(2)}) async-start(), calls=%async_computation.2 | async-start | bytes 4456448 | tf_op jit(solution)/shard_map/reduce_scatter | solution.py:509
  61.9 1.1 copy-start.4
  87.1 1.3 copy-start.3
  88.4 1.3 copy-start.5
  107.0 43.5 %copy-start = (bf16[16,128,256]{2,1,0:T(8,128)(2,1)S(1)}, bf16[16,128,256]{2,1,0:T(8,128)(2,1)}, u32[]{:S(2)}) copy-start(bf16[16,128,256]{2,1,0:T(8,128)(2,1)} %get-tuple-element.20.x_ref) | copy-start | bytes 3145732
Sparse Core Ops, SparseCore 0:
  50.7 36.3 all-gather.1
  89.6 58.1 reduce-scatter.1

commit v3 on v2

v3 whole, which is shorter than its diff:
```python
import functools
import math

import jax
import jax.numpy as jnp
from jax import lax
from jax.experimental import pallas as pl
from jax.experimental.pallas import tpu as pltpu
from jax.sharding import PartitionSpec as P

HD = 128
KVG = 8
HKEPT = 40
VGW = 4
CHUNK = 512

masked_score = -1e30
NT = (((1,), (1,)), ((), ()))
NN = (((1,), (0,)), ((), ()))


def matmul(a, b, dims):
    return lax.dot_general(a, b, dims, preferred_element_type=jnp.float32)


def fold_rows(x, op):
    rows, columns = x.shape
    return op(x.reshape(rows // 8, 8, columns), axis=0)


MESH = pl.DeviceIdType.MESH


def barrier_with(peers):
    barrier = pltpu.get_barrier_semaphore()
    for peer in peers:
        pl.semaphore_signal(barrier, inc=1, device_id=peer, device_id_type=MESH)
    pl.semaphore_wait(barrier, len(peers))


class Sender:
    def __init__(self, send_sems, recv_sems):
        self.send_sems, self.recv_sems, self.used = send_sems, recv_sems, 0

    def start(self, source, target, peer):
        copy = pltpu.make_async_remote_copy(
            src_ref=source,
            dst_ref=target,
            send_sem=self.send_sems.at[self.used],
            recv_sem=self.recv_sems.at[self.used],
            device_id=peer,
            device_id_type=MESH,
        )
        self.used += 1
        copy.start()
        return copy


def places():
    dp = lax.axis_index("dp")
    seq = lax.axis_index("seq")
    dps = lax.axis_size("dp")
    chips = lax.axis_size("seq") // 2
    z = seq // 2
    core = lax.rem(seq, 2)
    partner = (dp, 2 * z + 1 - core)

    def chip(offset):
        return (dp, 2 * lax.rem(z + offset + chips, chips) + core)

    def row(offset):
        return (lax.rem(dp + offset, dps), seq)

    return dp, seq, dps, chips, z, core, partner, chip, row


def gather_kernel(k_ref, v_ref, x_ref, kv_out, x_out, sends, recvs, local_sems):
    dp, seq, dps, chips, z, core, partner, chip, row = places()
    half = chips // 2
    width = k_ref.shape[1]
    parts = x_out.shape[2]
    barrier_with(
        [chip(1), chip(-1), partner] + [row(k) for k in range(1, dps)]
    )
    sender = Sender(sends, recvs)
    spans = (pl.ds(0, width), pl.ds(width, width))
    sources = (k_ref, v_ref)
    mine = kv_out.at[seq]
    flights = {}
    for part in range(2):
        for way in (1, -1):
            flights[part, way] = sender.start(
                sources[part], mine.at[:, spans[part]], chip(way)
            )
    passed = [
        sender.start(sources[part], mine.at[:, spans[part]], partner) for part in range(2)
    ]
    locals_ = [
        pltpu.make_async_copy(sources[part], mine.at[:, spans[part]], local_sems.at[part])
        for part in range(2)
    ] + [
        pltpu.make_async_copy(
            x_ref.at[:, pl.ds(pl.multiple_of(dp * parts, parts), parts)],
            x_out.at[dp], local_sems.at[2],
        ),
    ]
    for copy in locals_:
        copy.start()
    exchanged = []
    for k in range(1, dps):
        target = lax.rem(dp + k, dps)
        exchanged.append(
            sender.start(
                x_ref.at[:, pl.ds(pl.multiple_of(target * parts, parts), parts)],
                x_out.at[dp], row(k),
            )
        )
    sent = []
    for step in range(1, half + 1):
        for part in range(2):
            for way in (1, -1):
                last_way = 1 if part == 0 else -1
                if step == half and way != last_way:
                    continue
                copy = flights[part, way]
                copy.wait_recv()
                sent.append(copy)
                slot = 2 * lax.rem(z - way * step + chips, chips) + core
                block = kv_out.at[slot, :, spans[part]]
                if step < half - 1 or (step == half - 1 and way == last_way):
                    flights[part, way] = sender.start(block, block, chip(way))
                passed.append(sender.start(block, block, partner))
    for copy in locals_:
        copy.wait()
    for copy in passed + exchanged:
        copy.wait_recv()
    for copy in sent + passed + exchanged:
        copy.wait_send()


def gather_exchange(keys, values, layer_input):
    tokens, width = keys.shape
    dps = lax.axis_size("dp")
    members = lax.axis_size("seq")
    chips = members // 2
    parts = layer_input.shape[1] // dps
    copies = 4 * (chips // 2) + 4 * (chips // 2) + dps
    vmem = pl.BlockSpec(memory_space=pltpu.VMEM)
    return pl.pallas_call(
        gather_kernel,
        out_shape=(
            jax.ShapeDtypeStruct((members, tokens, 2 * width), jnp.bfloat16),
            jax.ShapeDtypeStruct((dps, tokens, parts), jnp.bfloat16),
        ),
        in_specs=[vmem] * 3,
        out_specs=(pl.BlockSpec(memory_space=pl.ANY), pl.BlockSpec(memory_space=pl.ANY)),
        scratch_shapes=[
            pltpu.SemaphoreType.DMA((copies,)),
            pltpu.SemaphoreType.DMA((copies,)),
            pltpu.SemaphoreType.DMA((3,)),
        ],
        compiler_params=pltpu.CompilerParams(collective_id=0, has_side_effects=True),
        name="gather_exchange",
    )(keys, values, layer_input)


class Ring:
    def __init__(self, sender, partial, pair_in, ring_in, ring_out, fin_out):
        self.sender, self.partial, self.pair_in = sender, partial, pair_in
        self.ring_in, self.ring_out, self.fin_out = ring_in, ring_out, fin_out
        _, _, _, self.chips, self.z, self.core, self.partner, self.chip, _ = places()
        self.half = pair_in.shape[2]
        self.quarter = self.half // 2
        self.tokens = fin_out.shape[1]
        self.flights, self.sent, self.arrived = {}, [], set()
        order = []
        for k in range(1, self.chips // 2):
            order += [-k, k]
        order += [self.chips // 2, 0]
        self.index_of = {offset % self.chips: i for i, offset in enumerate(order)}
        theirs = pl.ds(pl.multiple_of((1 - self.core) * self.half, self.half), self.half)
        self.paired = [
            sender.start(
                partial.at[self.at_chip(offset), :, theirs], pair_in.at[i], self.partner
            )
            for i, offset in enumerate(order)
        ]

    def at_chip(self, offset):
        return lax.rem(self.z + offset + 2 * self.chips, self.chips)

    def own_sum(self, offset, way_index, rows):
        i = self.index_of[offset % self.chips]
        if i not in self.arrived:
            self.paired[i].wait_recv()
            self.arrived.add(i)
        begin = way_index * self.quarter
        start = pl.multiple_of(self.core * self.half + begin, self.quarter)
        mine = self.partial[self.at_chip(offset), rows, pl.ds(start, self.quarter)]
        theirs = self.pair_in[i, rows, begin:begin + self.quarter]
        return mine.astype(jnp.float32) + theirs.astype(jnp.float32)

    def step(self, step):
        tokens = self.tokens
        for part in range(2):
            rows = slice(part * tokens, (part + 1) * tokens)
            for way_index, way in enumerate((1, -1)):
                value = self.own_sum(-way * (1 + step), way_index, rows)
                if step:
                    copy = self.flights[part, way]
                    copy.wait_recv()
                    self.sent.append(copy)
                    value = value + self.ring_in[way_index, part, step - 1].astype(jnp.float32)
                value = value.astype(jnp.bfloat16)
                if step < self.chips - 1:
                    self.ring_out[way_index, part, step] = value
                    self.flights[part, way] = self.sender.start(
                        self.ring_out.at[way_index, part, step],
                        self.ring_in.at[way_index, part, step],
                        self.chip(way),
                    )
                else:
                    begin = way_index * self.quarter
                    self.fin_out[part, :, begin:begin + self.quarter] = value

    def copies(self):
        return self.paired + self.sent


def reduce_kernel(
    dv_ref, dka_ref, dkb_ref, x_ref, dk_out, w_out,
    pairs, rings_in, rings_out, fins,
    v_all, w_part, w_pair, w_sum, w_in, w_fin, w_fin_in,
    sends, recvs, local_sem,
):
    dp, seq, dps, chips, z, core, partner, chip, row = places()
    tokens = fins.shape[2]
    width = dv_ref.shape[2]
    half = width // 2
    whalf = w_part.shape[2] // 2
    other = 1 - core
    barrier_with(
        [partner]
        + [chip(k) for k in range(1, chips)]
        + [row(k) for k in range(1, dps)]
    )
    sender = Sender(sends, recvs)
    value, key_a, key_b = [
        Ring(sender, ref, pairs.at[i], rings_in.at[i], rings_out.at[i], fins.at[i])
        for i, ref in enumerate((dv_ref, dka_ref, dkb_ref))
    ]
    mine_columns = pl.ds(pl.multiple_of(core * half, half), half)
    done = 0
    for step in range(chips):
        value.step(step)
        if step % 2 == 0 and done < chips - 5:
            key_a.step(done)
            key_b.step(done)
            done += 1
    v_mine = v_all.at[dp, :, mine_columns]
    kept = pltpu.make_async_copy(fins.at[0, core], v_mine, local_sem.at[0])
    kept.start()
    v_back = sender.start(fins.at[0, other], v_mine, partner)
    kept.wait()
    v_back.wait_recv()
    spread = [sender.start(v_all.at[dp], v_all.at[dp], row(k)) for k in range(1, dps)]
    for step in range(done, chips):
        key_a.step(step)
        key_b.step(step)
    k_kept, k_back = [], []
    for i in (1, 2):
        start = pl.multiple_of((i - 1) * width + core * half, half)
        target = dk_out.at[:, pl.ds(start, half)]
        k_kept.append(pltpu.make_async_copy(fins.at[i, core], target, local_sem.at[i]))
        k_kept[-1].start()
        k_back.append(sender.start(fins.at[i, other], target, partner))

    for copy in spread:
        copy.wait_recv()
    parts = x_ref.shape[2]
    joined = min(4, dps)

    def multiply(i, total):
        window = pl.ds(i * joined, joined)
        return total + lax.dot_general(
            x_ref[window].reshape(joined * tokens, parts),
            v_all[window].reshape(joined * tokens, width),
            (((0,), (0,)), ((), ())),
            preferred_element_type=jnp.float32,
        )

    total = lax.fori_loop(
        0, dps // joined, multiply, jnp.zeros((parts, width), jnp.float32)
    )
    w_part[...] = total.reshape(w_part.shape)
    w_mine = pl.multiple_of(core * whalf, whalf)
    w_other = pl.multiple_of(other * whalf, whalf)
    w_paired = sender.start(w_part.at[:, :, pl.ds(w_other, whalf)], w_pair, partner)
    for copy in k_kept:
        copy.wait()
    for copy in k_back:
        copy.wait_recv()
    w_paired.wait_recv()
    w_sum[...] = w_part[:, :, pl.ds(w_mine, whalf)] + w_pair[...]
    direct = [
        sender.start(w_sum.at[value.at_chip(k)], w_in.at[k - 1], chip(k))
        for k in range(1, chips)
    ]
    total = w_sum[z]
    for k, copy in enumerate(direct):
        copy.wait_recv()
        total = total + w_in[k]
    w_fin[...] = total.reshape(w_fin.shape)
    w_back = sender.start(w_fin.at[other], w_fin_in, partner)
    w_out[:, pl.ds(w_mine, whalf)] = w_fin[core]
    w_back.wait_recv()
    w_out[:, pl.ds(w_other, whalf)] = w_fin_in[...]
    copies = value.copies() + key_a.copies() + key_b.copies()
    for copy in copies + spread + direct + k_back + [v_back, w_paired, w_back]:
        copy.wait_send()


def reduce_exchange(dv, dka, dkb, input_parts):
    dps, tokens, parts = input_parts.shape
    members = lax.axis_size("seq")
    chips = members // 2
    width = dv.shape[1]
    owned = parts // members
    copies = 3 * (chips + 4 * (chips - 1)) + (dps - 1) + (chips - 1) + 5
    vmem = pl.BlockSpec(memory_space=pltpu.VMEM)
    bf, f32 = jnp.bfloat16, jnp.float32
    blocks = [x.reshape(chips, 2 * tokens, width) for x in (dv, dka, dkb)]
    return pl.pallas_call(
        reduce_kernel,
        out_shape=(
            jax.ShapeDtypeStruct((tokens, 2 * width), bf),
            jax.ShapeDtypeStruct((owned, width), f32),
        ),
        in_specs=[vmem] * 4,
        out_specs=(vmem, vmem),
        scratch_shapes=[
            pltpu.VMEM((3, chips, 2 * tokens, width // 2), bf),
            pltpu.VMEM((3, 2, 2, chips - 1, tokens, width // 4), bf),
            pltpu.VMEM((3, 2, 2, chips - 1, tokens, width // 4), bf),
            pltpu.VMEM((3, 2, tokens, width // 2), bf),
            pltpu.VMEM((dps, tokens, width), bf),
            pltpu.VMEM((chips, 2 * owned, width), f32),
            pltpu.VMEM((chips, 2 * owned, width // 2), f32),
            pltpu.VMEM((chips, 2 * owned, width // 2), f32),
            pltpu.VMEM((chips - 1, 2 * owned, width // 2), f32),
            pltpu.VMEM((2, owned, width // 2), f32),
            pltpu.VMEM((owned, width // 2), f32),
            pltpu.SemaphoreType.DMA((copies,)),
            pltpu.SemaphoreType.DMA((copies,)),
            pltpu.SemaphoreType.DMA((3,)),
        ],
        compiler_params=pltpu.CompilerParams(
            collective_id=1, has_side_effects=True, vmem_limit_bytes=48 * 1024 * 1024
        ),
        name="reduce_exchange",
    )(*blocks, input_parts)


def attention_kernel(
    base, with_value, info, q_ref, do_ref, k_ref, v_ref, *refs
):
    if base:
        dq_before, *refs = refs
    if with_value:
        dq_ref, dk_ref, dv_ref, *refs = refs
    else:
        dq_ref, dk_ref, *refs = refs
    qs, dos, s_scr, dp_scr, acc, kt_scr = refs
    if base:
        @pl.when(pl.program_id(0) == 0)
        def _():
            dq_ref[...] = dq_before[...]

    group = base + pl.program_id(0)
    block = info[2 * KVG]
    first_head = info[group]
    head_count = info[KVG + group]
    tokens = q_ref.shape[0]
    scaling = 1.0 / math.sqrt(HD)
    to_exp2 = scaling * math.log2(math.e)
    last = (block * tokens) // CHUNK
    row_base = block * tokens

    def rows_at(c):
        return pl.ds(pl.multiple_of(c * CHUNK, CHUNK), CHUNK)

    def prepare(c, _):
        rows = rows_at(c)
        kt_scr[:, rows] = k_ref[rows, :].T
        acc[rows, :] = jnp.zeros((CHUNK, acc.shape[1]), jnp.float32)
        return 0

    lax.fori_loop(0, last + 1, prepare, 0)

    def run_heads(head, count):
        width = count * tokens
        for i in range(count):
            columns = pl.ds(pl.multiple_of((head + i) * HD, HD), HD)
            qs[i * tokens:(i + 1) * tokens, :] = q_ref[:, columns]
            dos[i * tokens:(i + 1) * tokens, :] = do_ref[:, columns]
        q = qs[:width, :]
        do = dos[:width, :]

        def scores(c, top, masked):
            rows = rows_at(c)
            s = matmul(k_ref[rows, :], q, NT)
            if masked:
                key_at = c * CHUNK + lax.broadcasted_iota(jnp.int32, (CHUNK, width), 0)
                row_at = row_base + lax.rem(
                    lax.broadcasted_iota(jnp.int32, (CHUNK, width), 1), tokens
                )
                s = jnp.where(key_at <= row_at, s, masked_score)
            s_scr[rows, :width] = s
            return jnp.maximum(top, fold_rows(s, jnp.max))

        top = lax.fori_loop(
            0, last, lambda c, t: scores(c, t, False),
            jnp.full((8, width), masked_score, jnp.float32),
        )
        top = scores(last, top, True)
        shift = jnp.max(top, axis=0, keepdims=True) * to_exp2

        def weigh(c, carry):
            total, term = carry
            rows = rows_at(c)
            e = jnp.exp2(s_scr[rows, :width] * to_exp2 - shift)
            dp = matmul(v_ref[rows, :], do, NT)
            s_scr[rows, :width] = e
            dp_scr[rows, :width] = dp
            return (total + fold_rows(e, jnp.sum), term + fold_rows(e * dp, jnp.sum))

        zero = jnp.zeros((8, width), jnp.float32)
        total, term = lax.fori_loop(0, last + 1, weigh, (zero, zero))
        inverse = 1.0 / jnp.sum(total, axis=0, keepdims=True)
        row_term = jnp.sum(term, axis=0, keepdims=True) * inverse

        def grads(c, dqt):
            rows = rows_at(c)
            p = s_scr[rows, :width] * inverse
            ds = (p * (dp_scr[rows, :width] - row_term)).astype(jnp.bfloat16)
            if with_value:
                acc[rows, HD:] += matmul(p.astype(jnp.bfloat16), do, NN)
            acc[rows, :HD] += matmul(ds, q, NN)
            return dqt + matmul(kt_scr[:, rows], ds, NN)

        dqt = lax.fori_loop(0, last + 1, grads, jnp.zeros((HD, width), jnp.float32))
        dq = ((dqt * scaling).T).astype(dq_ref.dtype)
        for i in range(count):
            columns = pl.ds(pl.multiple_of((head + i) * HD, HD), HD)
            dq_ref[:, columns] = dq[i * tokens:(i + 1) * tokens, :]

    def pair(i, _):
        run_heads(first_head + 2 * i, 2)
        return 0

    lax.fori_loop(0, head_count // 2, pair, 0)

    @pl.when(head_count % 2 == 1)
    def _():
        run_heads(first_head + head_count - 1, 1)

    def finish(c, _):
        rows = rows_at(c)
        dk_ref[rows, :] = (acc[rows, :HD] * scaling).astype(dk_ref.dtype)
        if with_value:
            dv_ref[rows, :] = acc[rows, HD:].astype(dv_ref.dtype)
        return 0

    lax.fori_loop(0, last + 1, finish, 0)

    def clear(c, _):
        for ref in (dk_ref, dv_ref) if with_value else (dk_ref,):
            ref[rows_at(c), :] = jnp.zeros((CHUNK, HD), ref.dtype)
        return 0

    lax.fori_loop(last + 1, dk_ref.shape[0] // CHUNK, clear, 0)


def attention_grads(queries, grads, kv, info, base, with_value, before=None):
    tokens, width = queries.shape
    sequence, kv_width = kv.shape
    groups = VGW
    offset = kv_width // (2 * HD)
    wide = 2 * HD if with_value else HD
    whole = pl.BlockSpec((tokens, width), lambda g, info: (0, 0))
    key_block = pl.BlockSpec((sequence, HD), lambda g, info: (0, base + g))
    value_block = pl.BlockSpec((sequence, HD), lambda g, info: (0, offset + base + g))
    group_block = pl.BlockSpec((sequence, HD), lambda g, info: (0, g))
    given = () if before is None else (before,)
    return pl.pallas_call(
        functools.partial(attention_kernel, base, with_value),
        out_shape=(
            jax.ShapeDtypeStruct((tokens, width), jnp.bfloat16),
        ) + (jax.ShapeDtypeStruct((sequence, groups * HD), jnp.bfloat16),) * (wide // HD),
        grid_spec=pltpu.PrefetchScalarGridSpec(
            num_scalar_prefetch=1,
            grid=(groups,),
            in_specs=[whole, whole, key_block, value_block] + [whole] * len(given),
            out_specs=[whole] + [group_block] * (wide // HD),
            scratch_shapes=[
                pltpu.VMEM((2 * tokens, HD), jnp.bfloat16),
                pltpu.VMEM((2 * tokens, HD), jnp.bfloat16),
                pltpu.VMEM((sequence, 2 * tokens), jnp.float32),
                pltpu.VMEM((sequence, 2 * tokens), jnp.float32),
                pltpu.VMEM((sequence, wide), jnp.float32),
                pltpu.VMEM((HD, sequence), jnp.bfloat16),
            ],
        ),
        compiler_params=pltpu.CompilerParams(
            dimension_semantics=("arbitrary",), vmem_limit_bytes=48 * 1024 * 1024
        ),
        cost_estimate=pl.CostEstimate(
            flops=2 * 5 * HKEPT * tokens * sequence * HD,
            bytes_accessed=30 * 1024 * 1024,
            transcendentals=HKEPT * tokens * sequence,
        ),
        name="attention_grads",
    )(info, queries, grads, kv, kv, *given)


def local(query_states, key_states, value_states, output_grad, layer_input, head_counts):
    queries, grads = query_states[0], output_grad[0]
    group_ends = jnp.cumsum(head_counts)
    info = jnp.concatenate(
        [group_ends - head_counts, head_counts, lax.axis_index("seq").reshape(1)]
    ).astype(jnp.int32)
    kv, input_parts = gather_exchange(key_states[0], value_states[0], layer_input[0])
    kv = kv.reshape(-1, kv.shape[2])
    query_grad, dk_first, dv = attention_grads(queries, grads, kv, info, 0, True)
    query_grad, dk_late = attention_grads(queries, grads, kv, info, VGW, False, query_grad)
    key_grad, weight_grad = reduce_exchange(dv, dk_first, dk_late, input_parts)
    return (query_grad[None], key_grad[None], weight_grad)


def solution(mesh):
    placed = P("dp", "seq", None)
    return jax.shard_map(
        local,
        mesh=mesh,
        in_specs=(placed, placed, placed, placed, placed, P()),
        out_specs=(placed, placed, P(("dp", "seq"), None)),
        check_vma=False,
    )
```

time: 212 us -> 228 us (1.075)
  Pallas kernels: 122 us -> 221 us
  waiting for transfers between devices: 65 us -> 0 us
  between operations: 14.1 us -> 0.67 us
  local copies, waits for them, and re-layouts: 8.93 us -> 5.31 us
    pallas_call x1, Pallas kernels: 52.9 us -> 134 us  [reduce_exchange(): pl.pallas_call(reduce_kernel, out_shape=(jax.ShapeDtypeStruct((tokens, 2...]
    reduce_scatter x1 -> x0, waiting for transfers between devices: 40.9 us -> none  [local(): summed = lax.psum_scatter(dkv_first, 'seq', scatter_dimension=0, tiled=True)]
    all_gather x1 -> x0, waiting for transfers between devices: 24.1 us -> none  [local(): kv_late = lax.all_gather(kv_late, 'seq', axis=0, tiled=True)]
    pallas_call x1, Pallas kernels: 40.5 us -> 57 us  [gather_exchange(): pl.pallas_call(gather_kernel, out_shape=(jax.ShapeDtypeStruct((members, t...]
    slice x3 -> x0, local copies, waits for them, and re-layouts: 3.45 us -> none  [the longest x2 1.98 us: local(): kv_late = jnp.concatenate([keys[:, split:], values[:, split:]], axis=1)]
    unnamed x17 -> x12, local copies, waits for them, and re-layouts: 4.36 us -> 5.31 us
  transfers between devices with their start and end apart: 2 -> 0, of which waited for: 2 -> 0; matrix products, arithmetic and copies ran while one was open for 0% -> 0% of each run, Pallas kernels for 13% -> 0%
where the time goes in v3:
time: 228 us; the launch traced here: 229 us
  Pallas kernels  221 us (97%)
  local copies, waits for them, and re-layouts  5.31 us (2%)
    pallas_call x1, Pallas kernels, reduce_exchange(): pl.pallas_call(reduce_kernel, out_shape=(jax.ShapeDtypeStruct((tokens, 2...  134 us
    pallas_call x1, Pallas kernels, gather_exchange(): pl.pallas_call(gather_kernel, out_shape=(jax.ShapeDtypeStruct((members, t...  57 us
    pallas_call x2, Pallas kernels, attention_grads(): pl.pallas_call(functools.partial(attention_kernel, base, with_value), out...  29.7 us
    unnamed x12, local copies, waits for them, and re-layouts  5.31 us

profile of v3, /device:TPU:1, one launch (start us, length us, event | category | flops | bytes accessed | tf_op | source)
XLA Modules:
  0.0 228.7 jit_solution(13421580314071751483)
XLA Ops:
  0.6 0.8 reduce-window.9
  1.5 0.7 bitcast_subtract_fusion
  2.1 0.7 pad_add_fusion.info
  2.9 57.0 %gather_exchange.1 = (bf16[16,128,2048]{2,1,0:T(8,128)(2,1)}, bf16[16,128,256]{2,1,0:T(8,128)(2,1)}) custom-call(bf16[128,1024]{1,0:T(8,128)(2,1)} %bitcast.24, bf16[128,1024]{1,0:T(8,128)(2,1)} %bitcast.25, bf16[128,4096]{1,0:T(8,128)(2,1)} %bitcast.23), custom_call_target="tpu_custom_call" | custom-call | tf_op jit(solution)/shard_map/gather_exchange/pallas_call | solution.py:149
  59.9 0.0 copy-start.3
  59.9 1.3 copy-done.3
  61.2 0.0 copy-start.4
  61.2 1.3 copy-done.4
  62.5 17.0 %attention_grads.2 = (bf16[128,5120]{1,0:T(8,128)(2,1)S(1)}, bf16[2048,512]{1,0:T(8,128)(2,1)S(1)}, bf16[2048,512]{1,0:T(8,128)(2,1)}) custom-call(s32[17]{0:T(128)S(1)} %pad_add_fusion.info, bf16[128,5120]{1,0:T(8,128)(2,1)S(1)} %bitcast.19, bf16[128,5120]{1,0:T(8,128)(2,1)S(1)} %bitcast.21, bf16[2048,2048]{1,0:T(8,128)(2,1)} %bitcast.27, ...), custom_call_target="tpu_custom_call" | custom-call | flops 13421772800 | bytes 31457280 | tf_op jit(solution)/shard_map/attention_grads/pallas_call | solution.py:495
  79.5 0.0 copy-start
  79.5 0.0 copy-start.2
  79.5 12.7 %attention_grads.3 = (bf16[128,5120]{1,0:T(8,128)(2,1)}, bf16[2048,512]{1,0:T(8,128)(2,1)S(1)}) custom-call(s32[17]{0:T(128)S(1)} %pad_add_fusion.info, bf16[128,5120]{1,0:T(8,128)(2,1)S(1)} %bitcast.20, bf16[128,5120]{1,0:T(8,128)(2,1)S(1)} %bitcast.22, bf16[2048,2048]{1,0:T(8,128)(2,1)} %bitcast.29, bf16[2048,2048]{1,0:T(8,128)(2,1)} %bitcast.30, ...), custom_call_target="tpu_custom_call" | custom-call | flops 13421772800 | bytes 31457280 | tf_op jit(solution)/shard_map/attention_grads/pallas_call | solution.py:495
  92.2 0.0 copy-start.1
  92.2 1.4 copy-done.1
  93.6 0.0 copy-done
  93.6 0.0 copy-done.2
  93.6 133.8 %reduce_exchange.1 = (bf16[128,1024]{1,0:T(8,128)(2,1)S(1)}, f32[16,512]{1,0:T(8,128)S(1)}) custom-call(bf16[8,256,512]{2,1,0:T(8,128)(2,1)S(1)} %bitcast.16, bf16[8,256,512]{2,1,0:T(8,128)(2,1)S(1)} %bitcast.15, bf16[8,256,512]{2,1,0:T(8,128)(2,1)} %bitcast.17, bf16[16,128,256]{2,1,0:T(8,128)(2,1)S(1)} %copy-done.2), custom_call_target="tpu_custom_call" | custom-call | tf_op jit(solution)/shard_map/reduce_exchange/pallas_call | solution.py:333
  227.4 0.7 copy.11
  228.1 0.6 copy.12
Async XLA Ops:
  59.9 1.3 copy-start.3
  61.2 1.3 copy-start.4
  79.5 14.1 %copy-start = (bf16[2048,512]{1,0:T(8,128)(2,1)S(1)}, bf16[2048,512]{1,0:T(8,128)(2,1)}, u32[]{:S(2)}) copy-start(bf16[2048,512]{1,0:T(8,128)(2,1)} %get-tuple-element.15) | copy-start | bytes 6291460
  79.5 14.1 %copy-start.2 = (bf16[16,128,256]{2,1,0:T(8,128)(2,1)S(1)}, bf16[16,128,256]{2,1,0:T(8,128)(2,1)}, u32[]{:S(2)}) copy-start(bf16[16,128,256]{2,1,0:T(8,128)(2,1)} %get-tuple-element.18.x_ref) | copy-start | bytes 3145732
  92.2 1.4 copy-start.1
